TPU v7x, 32 devices: a whole 2x2x4 slice. The times are simulated.
32 devices in a mesh: tile: 8 (over y, x, core), gene: 4 (over z).
Axes of the slice: x: 2, y: 2, z: 4, core: 2. Of those that a mesh axis runs over, the one named last changes fastest.
Arguments:
- features: bfloat16 [64, 256, 1536], P('tile'), may hold values from -6 to 6
- counts: int32 [64, 256, 4096], P('tile', None, 'gene'), may hold values from 0 to 12
- selection: int32 [32, 4], P('gene'), may hold values from 0 to 11, as said below
- weights: bfloat16 [4608, 4096], P('tile', 'gene'), may hold values from -0.09375 to 0.09375
Outputs:
- grad_weights: float32 [4608, 4096], P('tile', 'gene')
Inputs may be any that keep to these rules, and one draw needn't show every extreme that they name: `selection`: each row names 4 different feature blocks.
All inputs are finite; a program needn't handle non-finite values.
Results may differ from a plain program's by a relative error of at most 0.0038.
Values may be sent and summed in bfloat16 or wider, within the bound.
No kernel may reach another device: no remote copies, remote signals or barrier semaphores. Data moves between devices by JAX's collectives and lax.ppermute only.
A program may use at most 576 MiB of HBM per device.

v0:
```python
import math

import jax
import jax.numpy as jnp
from jax import lax
from jax.sharding import PartitionSpec as P


def padded_2(block, sides, width):
    for axis, dim in sides:
        count = lax.axis_size(axis)
        forward = [(i, i + 1) for i in range(count - 1)]
        backward = [(target, source) for source, target in forward]
        low = lax.ppermute(
            lax.slice_in_dim(block, block.shape[dim] - width, None, axis=dim), axis, forward
        )
        high = lax.ppermute(lax.slice_in_dim(block, 0, width, axis=dim), axis, backward)
        block = jnp.concatenate([low, block, high], axis=dim)
    return block


def build_window(padded, chosen, row_count, col_count):
    col_blocks = [
        lax.dynamic_slice_in_dim(padded, chosen[feat_slot] * 128, 128, 2)
        for feat_slot in range(chosen.shape[0])
    ]
    pieces = []
    for row_step in (-1, 0, 1):
        for col_step in (-1, 0, 1):
            for col_block in col_blocks:
                pieces.append(
                    col_block[
                        1 + row_step : 1 + row_step + row_count,
                        1 + col_step : 1 + col_step + col_count,
                        :,
                    ]
                )
    return jnp.concatenate(pieces, axis=2).reshape(row_count * col_count, -1)


def per_device(features, counts, selection, weights):
    row_count, col_count, feat_width = features.shape
    local_genes = counts.shape[2]
    local_blocks = selection.shape[0]
    tile_count = lax.axis_size("tile")
    gene_total = local_genes * lax.axis_size("gene")
    norm_scale = 1.0 / math.sqrt(row_count * tile_count * col_count)
    bin_count = row_count * col_count
    partial_library = jnp.sum(counts.astype(jnp.float32), axis=2)
    library = lax.psum(partial_library, "gene") + 1.0
    size_factor = (library / gene_total).reshape(bin_count, 1)
    extended = padded_2(features, (("tile", 0),), 1)
    padded = jnp.pad(extended, ((0, 0), (1, 1), (0, 0)))
    windows = [
        build_window(padded, selection[gene_slot], row_count, col_count)
        for gene_slot in range(local_blocks)
    ]
    full_weights = lax.all_gather(weights, "tile", axis=0, tiled=True)
    products = []
    for gene_slot in range(local_blocks):
        columns = windows[gene_slot]
        products.append(
            jnp.dot(
                columns,
                full_weights[:, 128 * gene_slot : 128 * (gene_slot + 1)],
                preferred_element_type=jnp.float32,
            )
        )
    logits = jnp.concatenate(products, axis=1)
    observed = counts.reshape(bin_count, local_genes).astype(jnp.float32)
    excess = (size_factor * jnp.exp(logits) - observed).astype(jnp.bfloat16)
    share_rows = weights.shape[0]
    products = []
    for gene_slot in range(local_blocks):
        columns = windows[gene_slot]
        products.append(
            lax.dot_general(
                columns,
                excess[:, 128 * gene_slot : 128 * (gene_slot + 1)],
                (((0,), (0,)), ((), ())),
                preferred_element_type=jnp.float32,
            )
        )
    summed = lax.psum(jnp.concatenate(products, axis=1), "tile")
    own_rows = lax.dynamic_slice_in_dim(summed, lax.axis_index("tile") * share_rows, share_rows, 0)
    return own_rows * norm_scale


def solution(mesh):
    in_specs = (P("tile", None, None), P("tile", None, "gene"), P("gene", None), P("tile", "gene"))
    out_specs = P("tile", "gene")
    return jax.shard_map(
        per_device, mesh=mesh, in_specs=in_specs, out_specs=out_specs, check_vma=False
    )
```

profile of v0, /device:TPU:0, one launch (start us, length us, event | category | flops | bytes accessed | tf_op | source)
XLA Modules:
  0.0 707.2 jit_solution(11830557164873956825)
XLA Ops:
  36.5 8.6 %convert_element_type.12 = f32[8,256,1024]{2,1,0:T(8,128)} convert(s32[8,256,1024]{2,1,0:T(8,128)} %param.5) | non-fusion elementwise | flops 2097152 | bytes 16777216 | tf_op jit(solution)/shard_map/convert_element_type | solution.py:49
  45.1 9.5 %copy.24 = f32[2048,1024]{0,1:T(8,128)} copy(f32[2048,1024]{1,0:T(8,128)} %bitcast.60) | data formatting | bytes 16777216 | tf_op jit(solution)/shard_map/convert_element_type | solution.py:70
  58.6 12.7 %psum.14 = f32[8,256]{1,0:T(8,128)S(1)} all-reduce(f32[8,256]{1,0:T(8,128)S(1)} %convert_reduce_fusion), channel_id=1, replica_groups=mesh['tile'=8,'gene'=4] {'gene'}, use_global_device_ids=true, to_apply=%region_1.0 | all-reduce | flops 2048 | bytes 16384 | tf_op jit(solution)/shard_map/psum | solution.py:50
  71.6 5.6 fusion.5
  214.5 5.0 constant_dynamic-update-slice_fusion.255
  224.3 5.0 constant_dynamic-update-slice_fusion.253
  251.1 14.0 %convolution_dynamic-update-slice_fusion.15 = f32[2048,1024]{0,1:T(8,128)} fusion(bf16[2048,4608]{1,0:T(8,128)(2,1)} %bitcast.4, bf16[4608,1024]{1,0:T(8,128)(2,1)} %all-gather.2.cloned.1.call-done), kind=kOutput, calls=%fused_computation.24 | convolution fusion | flops 2415919104 | bytes 21102592 | tf_op jit(solution)/shard_map/dot_general | solution.py:63
  265.1 14.5 %convolution_dynamic-update-slice_fusion.14 = f32[2048,1024]{0,1:T(8,128)} fusion(f32[2048,1024]{0,1:T(8,128)} %convolution_dynamic-update-slice_fusion.15, bf16[2048,4608]{1,0:T(8,128)(2,1)} %bitcast.9, bf16[4608,1024]{1,0:T(8,128)(2,1)} %all-gather.2.cloned.1.call-done), kind=kOutput, calls=%fused_computation.23 | convolution fusion | flops 2415919104 | bytes 21102592 | tf_op jit(solution)/shard_map/dot_general | solution.py:63
  279.6 14.0 %convolution_dynamic-update-slice_fusion.13 = f32[2048,1024]{0,1:T(8,128)} fusion(f32[2048,1024]{0,1:T(8,128)} %convolution_dynamic-update-slice_fusion.14, bf16[2048,4608]{1,0:T(8,128)(2,1)} %bitcast.14, bf16[4608,1024]{1,0:T(8,128)(2,1)} %all-gather.2.cloned.1.call-done), kind=kOutput, calls=%fused_computation.22 | convolution fusion | flops 2415919104 | bytes 21102592 | tf_op jit(solution)/shard_map/dot_general | solution.py:63
  293.5 14.0 %convolution_dynamic-update-slice_fusion.12 = f32[2048,1024]{0,1:T(8,128)} fusion(f32[2048,1024]{0,1:T(8,128)} %convolution_dynamic-update-slice_fusion.13, bf16[2048,4608]{1,0:T(8,128)(2,1)} %bitcast.19, bf16[4608,1024]{1,0:T(8,128)(2,1)} %all-gather.2.cloned.1.call-done), kind=kOutput, calls=%fused_computation.21 | convolution fusion | flops 2415919104 | bytes 21102592 | tf_op jit(solution)/shard_map/dot_general | solution.py:63
  307.5 14.0 %convolution_dynamic-update-slice_fusion.11 = f32[2048,1024]{0,1:T(8,128)} fusion(f32[2048,1024]{0,1:T(8,128)} %convolution_dynamic-update-slice_fusion.12, bf16[2048,4608]{1,0:T(8,128)(2,1)} %bitcast.24, bf16[4608,1024]{1,0:T(8,128)(2,1)} %all-gather.2.cloned.1.call-done), kind=kOutput, calls=%fused_computation.20 | convolution fusion | flops 2415919104 | bytes 21102592 | tf_op jit(solution)/shard_map/dot_general | solution.py:63
  321.5 14.1 %convolution_dynamic-update-slice_fusion.10 = f32[2048,1024]{0,1:T(8,128)} fusion(f32[2048,1024]{0,1:T(8,128)} %convolution_dynamic-update-slice_fusion.11, bf16[2048,4608]{1,0:T(8,128)(2,1)} %bitcast.29, bf16[4608,1024]{1,0:T(8,128)(2,1)} %all-gather.2.cloned.1.call-done), kind=kOutput, calls=%fused_computation.19 | convolution fusion | flops 2415919104 | bytes 21102592 | tf_op jit(solution)/shard_map/dot_general | solution.py:63
  335.6 14.0 %convolution_dynamic-update-slice_fusion.9 = f32[2048,1024]{0,1:T(8,128)} fusion(f32[2048,1024]{0,1:T(8,128)} %convolution_dynamic-update-slice_fusion.10, bf16[2048,4608]{1,0:T(8,128)(2,1)} %bitcast.34, bf16[4608,1024]{1,0:T(8,128)(2,1)} %all-gather.2.cloned.1.call-done), kind=kOutput, calls=%fused_computation.18 | convolution fusion | flops 2415919104 | bytes 21102592 | tf_op jit(solution)/shard_map/dot_general | solution.py:63
  349.7 14.0 %convolution_dynamic-update-slice_fusion.8 = f32[2048,1024]{0,1:T(8,128)} fusion(f32[2048,1024]{0,1:T(8,128)} %convolution_dynamic-update-slice_fusion.9, bf16[2048,4608]{1,0:T(8,128)(2,1)} %bitcast.39, bf16[4608,1024]{1,0:T(8,128)(2,1)} %all-gather.2.cloned.1.call-done), kind=kOutput, calls=%fused_computation.17 | convolution fusion | flops 2415919104 | bytes 21102592 | tf_op jit(solution)/shard_map/dot_general | solution.py:63
  363.7 8.1 %subtract_convert_fusion = bf16[2048,1024]{0,1:T(8,128)(2,1)S(1)} fusion(f32[2048,1024]{0,1:T(8,128)} %copy.24, f32[2048,1024]{0,1:T(8,128)} %convolution_dynamic-update-slice_fusion.8, f32[2048]{0:T(1024)S(1)} %bitcast.61), kind=kLoop, calls=%fused_computation.6 | loop fusion | flops 6291456 | bytes 20979712 | tf_op jit(solution)/shard_map/convert_element_type | solution.py:71
  371.8 10.7 %convolution_dynamic-update-slice_fusion.7 = f32[4608,1024]{1,0:T(8,128)} fusion(bf16[2048,4608]{1,0:T(8,128)(2,1)} %bitcast.4, bf16[2048,1024]{0,1:T(8,128)(2,1)S(1)} %subtract_convert_fusion), kind=kOutput, calls=%fused_computation.16 | convolution fusion | flops 2415919104 | bytes 21757952 | tf_op jit(solution)/shard_map/dot_general | solution.py:77
  382.5 10.5 %convolution_dynamic-update-slice_fusion.6 = f32[4608,1024]{1,0:T(8,128)} fusion(f32[4608,1024]{1,0:T(8,128)} %convolution_dynamic-update-slice_fusion.7, bf16[2048,4608]{1,0:T(8,128)(2,1)} %bitcast.9, bf16[2048,1024]{0,1:T(8,128)(2,1)S(1)} %subtract_convert_fusion), kind=kOutput, calls=%fused_computation.15 | convolution fusion | flops 2415919104 | bytes 21757952 | tf_op jit(solution)/shard_map/dot_general | solution.py:77
  393.0 10.5 %convolution_dynamic-update-slice_fusion.5 = f32[4608,1024]{1,0:T(8,128)} fusion(f32[4608,1024]{1,0:T(8,128)} %convolution_dynamic-update-slice_fusion.6, bf16[2048,4608]{1,0:T(8,128)(2,1)} %bitcast.14, bf16[2048,1024]{0,1:T(8,128)(2,1)S(1)} %subtract_convert_fusion), kind=kOutput, calls=%fused_computation.14 | convolution fusion | flops 2415919104 | bytes 21757952 | tf_op jit(solution)/shard_map/dot_general | solution.py:77
  403.5 10.5 %convolution_dynamic-update-slice_fusion.4 = f32[4608,1024]{1,0:T(8,128)} fusion(f32[4608,1024]{1,0:T(8,128)} %convolution_dynamic-update-slice_fusion.5, bf16[2048,4608]{1,0:T(8,128)(2,1)} %bitcast.19, bf16[2048,1024]{0,1:T(8,128)(2,1)S(1)} %subtract_convert_fusion), kind=kOutput, calls=%fused_computation.13 | convolution fusion | flops 2415919104 | bytes 21757952 | tf_op jit(solution)/shard_map/dot_general | solution.py:77
  414.0 10.7 %convolution_dynamic-update-slice_fusion.3 = f32[4608,1024]{1,0:T(8,128)} fusion(f32[4608,1024]{1,0:T(8,128)} %convolution_dynamic-update-slice_fusion.4, bf16[2048,4608]{1,0:T(8,128)(2,1)} %bitcast.24, bf16[2048,1024]{0,1:T(8,128)(2,1)S(1)} %subtract_convert_fusion), kind=kOutput, calls=%fused_computation.12 | convolution fusion | flops 2415919104 | bytes 21757952 | tf_op jit(solution)/shard_map/dot_general | solution.py:77
  424.7 10.5 %convolution_dynamic-update-slice_fusion.2 = f32[4608,1024]{1,0:T(8,128)} fusion(f32[4608,1024]{1,0:T(8,128)} %convolution_dynamic-update-slice_fusion.3, bf16[2048,4608]{1,0:T(8,128)(2,1)} %bitcast.29, bf16[2048,1024]{0,1:T(8,128)(2,1)S(1)} %subtract_convert_fusion), kind=kOutput, calls=%fused_computation.11 | convolution fusion | flops 2415919104 | bytes 21757952 | tf_op jit(solution)/shard_map/dot_general | solution.py:77
  435.2 10.5 %convolution_dynamic-update-slice_fusion.1 = f32[4608,1024]{1,0:T(8,128)} fusion(f32[4608,1024]{1,0:T(8,128)} %convolution_dynamic-update-slice_fusion.2, bf16[2048,4608]{1,0:T(8,128)(2,1)} %bitcast.34, bf16[2048,1024]{0,1:T(8,128)(2,1)S(1)} %subtract_convert_fusion), kind=kOutput, calls=%fused_computation.10 | convolution fusion | flops 2415919104 | bytes 21757952 | tf_op jit(solution)/shard_map/dot_general | solution.py:77
  445.7 10.5 %convolution_dynamic-update-slice_fusion = f32[4608,1024]{1,0:T(8,128)} fusion(f32[4608,1024]{1,0:T(8,128)} %convolution_dynamic-update-slice_fusion.1, bf16[2048,4608]{1,0:T(8,128)(2,1)} %bitcast.39, bf16[2048,1024]{0,1:T(8,128)(2,1)S(1)} %subtract_convert_fusion), kind=kOutput, calls=%fused_computation.9 | convolution fusion | flops 2415919104 | bytes 21757952 | tf_op jit(solution)/shard_map/dot_general | solution.py:77
  456.2 240.3 %all-reduce.3.cloned.1.call-done = f32[4608,1024]{1,0:T(8,128)} async-done(((f32[4608,1024]{1,0:T(8,128)}), f32[4608,1024]{1,0:T(8,128)}) %all-reduce.3.cloned.1.call-update) | async-done | bytes 18874384 | tf_op jit(solution)/shard_map/psum | solution.py:84
  (101 shorter events, 181.4 us)
Async XLA Ops:
  6.5 244.6 %all-gather.2.cloned.1.call-start = ((), (), s32[]{:S(2)}) async-start(), calls=%async_computation | async-start | bytes 10616832 | tf_op jit(solution)/shard_map/all_gather | solution.py:58
  7.3 689.3 %all-reduce.3.cloned.1.call-start = ((), (), s32[]{:S(2)}) async-start(), calls=%async_computation.1 | async-start | bytes 37748736 | tf_op jit(solution)/shard_map/psum | solution.py:84
  8.8 62.8 %collective-permute-start = (bf16[1,256,1536]{2,1,0:T(8,128)(2,1)S(1)}, bf16[1,256,1536]{2,1,0:T(8,128)(2,1)S(1)}, u32[]{:S(2)}, u32[]{:S(2)}) collective-permute-start(bf16[1,256,1536]{2,1,0:T(8,128)(2,1)S(1)} %get-tuple-element.261), channel_id=1, source_target_pairs={{0,4},{4,8},{8,12},{12,16},{16,20},{20,24},{24,28},{1,5},{5,9},{9,... | collective-permute-start | bytes 2359304 | tf_op jit(solution)/shard_map/ppermute | solution.py:14
  11.2 60.3 %collective-permute-start.1 = (bf16[1,256,1536]{2,1,0:T(8,128)(2,1)S(1)}, bf16[1,256,1536]{2,1,0:T(8,128)(2,1)S(1)}, u32[]{:S(2)}, u32[]{:S(2)}) collective-permute-start(bf16[1,256,1536]{2,1,0:T(8,128)(2,1)S(1)} %get-tuple-element.262), channel_id=1, source_target_pairs={{4,0},{8,4},{12,8},{16,12},{20,16},{24,20},{28,24},{5,1},{9,5},{13... | collective-permute-start | bytes 2359304 | tf_op jit(solution)/shard_map/ppermute | solution.py:17
Sparse Core Ops, SparseCore 0:
  9.2 70.7 all-gather.1
  456.3 240.1 all-reduce.2
where the time goes:
time: 711 us; the launch traced here: 707 us
  waiting for transfers between devices  241 us (34%)
  matrix products  197 us (28%)
  local copies, waits for them, and re-layouts  189 us (27%)
  between operations  34.1 us (5%)
  other arithmetic  29.8 us (4%)
  blocking collectives  12.7 us (2%)
    psum x1, waiting for transfers between devices, per_device(): summed = lax.psum(jnp.concatenate(products, axis=1), 'tile')  240 us
    unnamed x86, local copies, waits for them, and re-layouts  165 us
    dot_general x8, matrix products, per_device(): jnp.dot(columns, full_weights[:, 128 * gene_slot:128 * (gene_slot + 1)],...  113 us
    dot_general x8, matrix products, per_device(): lax.dot_general(columns, excess[:, 128 * gene_slot:128 * (gene_slot + 1)]...  84.4 us
  transfers between devices with their start and end apart: 4, of which 1 were waited for; matrix products, arithmetic and copies ran while one was open for 29% of the time, Pallas kernels for 0%

commit v1 on v0

v1 whole, which is shorter than its diff:
```python
import functools
import math

import jax
import jax.numpy as jnp
from jax import lax
from jax.experimental import pallas as pl
from jax.experimental.pallas import tpu as pltpu
from jax.sharding import PartitionSpec as P


LANES = 128
STEPS = 3
ROUTES = ("direct", "direct", "x", "y")

NT = (((1,), (1,)), ((), ()))
KERNEL_VMEM = pltpu.CompilerParams(vmem_limit_bytes=24_000_000)
ALL_VMEM = pltpu.CompilerParams(vmem_limit_bytes=66_000_000)
HBM = pl.BlockSpec(memory_space=pltpu.HBM)
VMEM = pl.BlockSpec(memory_space=pltpu.VMEM)
SMEM = pl.BlockSpec(memory_space=pltpu.SMEM)
ANY = pl.BlockSpec(memory_space=pl.ANY)


def swap_cores(x, count):
    return lax.ppermute(x, "tile", [(t, t ^ 1) for t in range(count)])


def identity(dtype):
    rows = lax.broadcasted_iota(jnp.int32, (LANES, LANES), 0)
    cols = lax.broadcasted_iota(jnp.int32, (LANES, LANES), 1)
    return (rows == cols).astype(jnp.float32).astype(dtype)


def turned(x):
    return lax.dot_general(identity(x.dtype), x, NT, preferred_element_type=jnp.float32)


def counts_kernel(scalars, counts_ref, mine_ref, other_ref, library_ref):
    genes = mine_ref.shape[1]
    total = None
    for side, target in ((scalars[0], mine_ref), (1 - scalars[0], other_ref)):
        part = counts_ref[0, :, pl.ds(pl.multiple_of(side * genes, genes), genes)]
        target[...] = part.astype(jnp.float32).astype(jnp.bfloat16)
        for g in range(0, genes, LANES):
            total = part[:, :LANES] if total is None else total + part[:, g : g + LANES]
    ones = jnp.ones((8, LANES), jnp.bfloat16)
    total = total.astype(jnp.float32).astype(jnp.bfloat16)
    library_ref[...] = lax.dot_general(ones, total, NT, preferred_element_type=jnp.float32)[:1]


def small_counts(scalars, counts):
    row_count, col_count, genes = counts.shape
    bins = row_count * col_count
    small = pl.BlockSpec((col_count, genes // 2), lambda r, s: (r, 0))
    return pl.pallas_call(
        counts_kernel,
        grid_spec=pltpu.PrefetchScalarGridSpec(
            num_scalar_prefetch=1,
            grid=(row_count,),
            in_specs=[pl.BlockSpec((1, col_count, genes), lambda r, s: (r, 0, 0))],
            out_specs=[small, small, pl.BlockSpec((1, col_count), lambda r, s: (0, r))],
        ),
        out_shape=[jax.ShapeDtypeStruct((bins, genes // 2), jnp.bfloat16)] * 2
        + [jax.ShapeDtypeStruct((1, bins), jnp.float32)],
        compiler_params=ALL_VMEM,
        name="small_counts",
        cost_estimate=pl.CostEstimate(flops=0, bytes_accessed=counts.size * 6, transcendentals=0),
    )(scalars, counts)


def weights_kernel(scalars, mine_ref, came_ref, *rest):
    parts, rows = rest[:-1], rest[-1]
    core = scalars[0]
    share, genes = mine_ref.shape[0], rows.shape[1]
    lanes = pl.ds(pl.multiple_of(core * genes, genes), genes)
    rows[pl.ds(pl.multiple_of(core * share, 16), share), :] = mine_ref[:, lanes]
    rows[pl.ds(pl.multiple_of((1 - core) * share, 16), share), :] = came_ref[:, lanes]
    for j, part in enumerate(parts):
        for b in range(rows.shape[0] // LANES):
            block = rows[b * LANES : (b + 1) * LANES, j * LANES : (j + 1) * LANES]
            part[b] = turned(block).astype(jnp.bfloat16)


def turn_weights(scalars, mine, came):
    share, genes = mine.shape
    blocks = genes // 2 // LANES
    part = jax.ShapeDtypeStruct((2 * share // LANES, LANES, LANES), jnp.bfloat16)
    return pl.pallas_call(
        weights_kernel,
        in_specs=[SMEM, VMEM, VMEM],
        out_specs=[VMEM] * blocks,
        out_shape=[part] * blocks,
        scratch_shapes=[pltpu.VMEM((2 * share, genes // 2), jnp.bfloat16)],
        compiler_params=ALL_VMEM,
        name="turn_weights",
        cost_estimate=pl.CostEstimate(flops=0, bytes_accessed=mine.size * 6, transcendentals=0),
    )(scalars, mine, came)


def block_copies(own_rows, cols, block, scalars, selection, features, halos, counts, fs, cs, f_sem, c_sem):
    core, parity = scalars[0], scalars[2]
    own_bins = own_rows * cols
    reads = selection.shape[1]
    row = core * (selection.shape[0] // 2) + block
    half_blocks = halos[0].shape[1] // LANES
    spans = ((0, cols), (cols, own_bins), (cols + own_bins, own_bins), (cols + 2 * own_bins, cols))

    def feature_copy(place, k, source, feature_block):
        at, size = spans[place]
        lanes = pl.ds(pl.multiple_of(feature_block * LANES, LANES), LANES)
        return pltpu.make_async_copy(
            source.at[:, lanes], fs.at[pl.ds(at, size), pl.ds(k * LANES, LANES)], f_sem.at[place, k]
        )

    def count_copy(side, source):
        return pltpu.make_async_copy(
            source.at[:, pl.ds(block * LANES, LANES)], cs.at[pl.ds(side * own_bins, own_bins)], c_sem.at[side]
        )

    for this in range(2):

        @pl.when(core == this)
        def _():
            near, far = features if this == 0 else features[::-1]
            top, bottom = (halos[:2], halos[2:]) if this == 0 else (halos[2:], halos[:2])
            for k in range(reads):
                chosen = selection[row, k]
                feature_copy(1, k, near, chosen).start()
                feature_copy(2, k, far, chosen).start()
                upper = jnp.where(chosen >= half_blocks, 1, 0)
                for held in range(2):

                    @pl.when((upper == parity) == (held == 0))
                    def _():
                        feature_copy(0, k, top[held], chosen - upper * half_blocks).start()
                        feature_copy(3, k, bottom[held], chosen - upper * half_blocks).start()

            for side, source in enumerate(counts if this == 0 else counts[::-1]):
                count_copy(side, source).start()

    def wait():
        for place in range(4):
            for k in range(reads):
                feature_copy(place, k, features[0] if 0 < place < 3 else halos[0], 0).wait()
        for side in range(2):
            count_copy(side, counts[0]).wait()

    return wait


def load_kernel(plan, scalars, selection, *rest):
    own_rows, cols, block, gene_total = plan
    features, halos, counts, libraries, rest = rest[:2], rest[2:6], rest[6:8], rest[8], rest[9:]
    fs, cs, ls, f_sem, c_sem = rest
    wait = block_copies(own_rows, cols, block, scalars, selection, features, halos, counts, fs, cs, f_sem, c_sem)
    own_bins = own_rows * cols
    core = scalars[0]
    total = libraries[0]
    for i in range(1, libraries.shape[0]):
        total += libraries[i]
    sizes = (total + 1.0) / gene_total
    ls[:, pl.ds(pl.multiple_of(core * own_bins, own_bins), own_bins)] = sizes[:1]
    ls[:, pl.ds(pl.multiple_of((1 - core) * own_bins, own_bins), own_bins)] = sizes[1:]
    wait()


def loaded(bins, cols, reads):
    return [
        pltpu.VMEM((bins + 2 * cols, reads * LANES), jnp.bfloat16),
        pltpu.VMEM((bins, LANES), jnp.bfloat16),
    ]


def load_block(scalars, selection, features, halos, counts, libraries, block, own_rows, cols, gene_total):
    bins, reads = 2 * own_rows * cols, selection.shape[1]
    return pl.pallas_call(
        functools.partial(load_kernel, (own_rows, cols, block, gene_total)),
        in_specs=[SMEM] * 2 + [HBM] * 8 + [VMEM],
        out_specs=[VMEM] * 3,
        out_shape=loaded(bins, cols, reads) + [pltpu.VMEM((1, bins), jnp.float32)],
        scratch_shapes=[pltpu.SemaphoreType.DMA((4, reads)), pltpu.SemaphoreType.DMA((2,))],
        compiler_params=KERNEL_VMEM,
        name="load_block",
        cost_estimate=pl.CostEstimate(flops=0, bytes_accessed=12 * 2**20, transcendentals=0),
    )(scalars, selection, *features, *halos, *counts, libraries)


def grad_kernel(plan, scalars, selection, fs, cs, ls, *rest):
    own_rows, cols, following, pieces, piece_blocks = plan
    features, halos, counts, rest = rest[:2], rest[2:6], rest[6:8], rest[8:]
    w_parts, g_parts, rest = rest[:pieces], rest[pieces : 2 * pieces], rest[2 * pieces :]
    wait_next = None
    if following is not None:
        next_fs, next_cs, rest = rest[0], rest[1], rest[2:]
    wv, wl, et, acc, gb, f_sem, c_sem, w_sem, out_sem = rest
    rows = 2 * own_rows
    reads = selection.shape[1]

    def first_block(p):
        return (scalars[1] ^ p) * piece_blocks if pieces > 1 else 0

    weight_copies = [
        pltpu.make_async_copy(w_parts[p], wv.at[pl.ds(first_block(p), piece_blocks)], w_sem.at[p])
        for p in range(pieces)
    ]
    for copy in weight_copies:
        copy.start()
    if following is not None:
        wait_next = block_copies(
            own_rows, cols, following, scalars, selection, features, halos, counts, next_fs, next_cs, f_sem, c_sem
        )
    for copy in weight_copies:
        copy.wait()
    for d in range(STEPS):
        for e in range(STEPS):
            for k in range(reads):
                wl[d, e * LANES : (e + 1) * LANES, k * LANES : (k + 1) * LANES] = wv[(STEPS * d + e) * reads + k]

    lane = lax.broadcasted_iota(jnp.int32, (LANES, cols), 1)

    def from_left(x):
        return jnp.where(lane > 0, pltpu.roll(x, 1, 1), 0.0)

    def from_right(x):
        return jnp.where(lane < cols - 1, pltpu.roll(x, cols - 1, 1), 0.0)

    def products(r):
        total = None
        for d in range(STEPS):
            one = lax.dot_general(
                wl[d], fs[pl.ds((r + d) * cols, cols), :], NT, preferred_element_type=jnp.float32
            )
            total = one if total is None else total + one
        return total

    def finish(r, sums):
        here = slice(r * cols, (r + 1) * cols)
        logits = from_left(sums[:LANES]) + sums[LANES : 2 * LANES] + from_right(sums[2 * LANES :])
        excess = ls[:, here] * jnp.exp(logits) - turned(cs[here, :])
        et[:LANES, here] = from_right(excess).astype(jnp.bfloat16)
        et[LANES : 2 * LANES, here] = excess.astype(jnp.bfloat16)
        et[2 * LANES :, here] = from_left(excess).astype(jnp.bfloat16)

    acc[0] = products(0)
    for r in range(1, rows):
        acc[r % 2] = products(r)
        finish(r - 1, acc[(r - 1) % 2])
    finish(rows - 1, acc[(rows - 1) % 2])

    def row_step(d, carry):
        span = pl.ds(pl.multiple_of(d * cols, cols), rows * cols)
        grad = jnp.dot(et[...], fs[span, :], preferred_element_type=jnp.float32)
        for e in range(STEPS):
            for k in range(reads):
                gb[(STEPS * d + e) * reads + k] = grad[
                    e * LANES : (e + 1) * LANES, k * LANES : (k + 1) * LANES
                ].astype(jnp.bfloat16)
        return carry

    lax.fori_loop(0, STEPS, row_step, 0)

    stores = [
        pltpu.make_async_copy(gb.at[pl.ds(first_block(p), piece_blocks)], g_parts[p], out_sem.at[p])
        for p in range(pieces)
    ]
    for copy in stores:
        copy.start()
    if wait_next is not None:
        wait_next()
    for copy in stores:
        copy.wait()


def block_gradient(scalars, selection, held, features, halos, counts, w_parts, following, own_rows, cols):
    pieces = len(w_parts)
    piece_blocks = w_parts[0].shape[0]
    reads = selection.shape[1]
    rows = 2 * own_rows
    taps = STEPS * STEPS * reads
    bins = rows * cols
    plan = (own_rows, cols, following, pieces, piece_blocks)
    more = [] if following is None else loaded(bins, cols, reads)
    part = pltpu.HBM((piece_blocks, LANES, LANES), jnp.bfloat16)
    return pl.pallas_call(
        functools.partial(grad_kernel, plan),
        in_specs=[SMEM] * 2 + [VMEM] * 3 + [HBM] * 8 + [ANY] * pieces,
        out_specs=[HBM] * pieces + [VMEM] * len(more),
        scratch_shapes=[
            pltpu.VMEM((taps, LANES, LANES), jnp.bfloat16),
            pltpu.VMEM((STEPS, STEPS * LANES, reads * LANES), jnp.bfloat16),
            pltpu.VMEM((STEPS * LANES, bins), jnp.bfloat16),
            pltpu.VMEM((2, STEPS * LANES, cols), jnp.float32),
            pltpu.VMEM((taps, LANES, LANES), jnp.bfloat16),
            pltpu.SemaphoreType.DMA((4, reads)),
            pltpu.SemaphoreType.DMA((2,)),
            pltpu.SemaphoreType.DMA((pieces,)),
            pltpu.SemaphoreType.DMA((pieces,)),
        ],
        out_shape=[part] * pieces + more,
        compiler_params=KERNEL_VMEM,
        name="block_gradient",
        cost_estimate=pl.CostEstimate(
            flops=4 * taps * LANES * LANES * bins, bytes_accessed=10 * 2**20, transcendentals=LANES * bins
        ),
    )(scalars, selection, *held, *features, *halos, *counts, *w_parts)


def sum_kernel(scale, scalars, *rest):
    parts, (mine_ref, other_ref, rows) = rest[:-3], rest[-3:]
    core = scalars[0]
    share = mine_ref.shape[0]
    for b in range(parts[0].shape[0]):
        total = parts[0][b].astype(jnp.float32)
        for part in parts[1:]:
            total += part[b].astype(jnp.float32)
        rows[b * LANES : (b + 1) * LANES, :] = total.T * scale
    mine_ref[...] = rows[pl.ds(pl.multiple_of(core * share, 8), share), :]
    other_ref[...] = rows[pl.ds(pl.multiple_of((1 - core) * share, 8), share), :]


def summed(scalars, parts, share, scale):
    shape = jax.ShapeDtypeStruct((share, LANES), jnp.float32)
    return pl.pallas_call(
        functools.partial(sum_kernel, scale),
        in_specs=[SMEM] + [VMEM] * len(parts),
        out_specs=[VMEM] * 2,
        out_shape=[shape, shape],
        scratch_shapes=[pltpu.VMEM((2 * share, LANES), jnp.float32)],
        compiler_params=ALL_VMEM,
        name="summed",
        cost_estimate=pl.CostEstimate(flops=0, bytes_accessed=8 * share * LANES, transcendentals=0),
    )(scalars, *parts)


def place_kernel(base, aliased, scalars, *rest):
    parts, out, sem = rest[aliased:-2], rest[-2], rest[-1]
    core = scalars[0]
    core_genes = out.shape[1] // 2
    copies = []
    for i, part in enumerate(parts):
        side = core if i % 2 == 0 else 1 - core
        lanes = pl.ds(pl.multiple_of(side * core_genes + (base + i // 2) * LANES, LANES), LANES)
        copies.append(pltpu.make_async_copy(part, out.at[:, lanes], sem.at[i]))
    for copy in copies:
        copy.start()
    for copy in copies:
        copy.wait()


def placed(scalars, parts, base, out, share, genes):
    held = [] if out is None else [out]
    return pl.pallas_call(
        functools.partial(place_kernel, base, len(held)),
        in_specs=[SMEM] + [HBM] * len(held) + [VMEM] * len(parts),
        out_specs=HBM,
        out_shape=jax.ShapeDtypeStruct((share, genes), jnp.float32),
        scratch_shapes=[pltpu.SemaphoreType.DMA((len(parts),))],
        input_output_aliases={1: 0} if held else {},
        compiler_params=ALL_VMEM,
        name="placed",
        cost_estimate=pl.CostEstimate(flops=0, bytes_accessed=8 * share * LANES * len(parts), transcendentals=0),
    )(scalars, *held, *parts)


def exchanged(x, piece, count):
    return lax.ppermute(x, "tile", [(t, t ^ (2 * piece)) for t in range(count)])


def per_device(features, counts, selection, weights):
    row_count, col_count, width = features.shape
    local_genes = counts.shape[2]
    tiles, gene_parts = lax.axis_size("tile"), lax.axis_size("gene")
    gene_total = local_genes * gene_parts
    norm_scale = 1.0 / math.sqrt(row_count * tiles * col_count)
    bins = row_count * col_count
    me, gene_part = lax.axis_index("tile"), lax.axis_index("gene")
    core, chip, parity = me & 1, me >> 1, gene_part & 1
    scalars = jnp.stack([core, chip, parity]).astype(jnp.int32)
    core_genes = local_genes // 2
    core_blocks = core_genes // LANES
    share = weights.shape[0]
    chips = tiles // 2
    planned = chips == 4 and (2 * share) % LANES == 0 and len(ROUTES) == core_blocks

    flat = features.reshape(bins, width)
    if planned:
        came = swap_cores(weights, tiles)
    edge = lax.dynamic_slice(
        features, (core * (row_count - 1), 0, parity * (width // 2)), (1, col_count, width // 2)
    ).reshape(col_count, width // 2)
    outward = [(t, t + 1) for t in range(1, tiles - 1, 2)] + [(t, t - 1) for t in range(2, tiles, 2)]
    beside = [(g, g ^ 1) for g in range(gene_parts)]
    halo = lax.ppermute(edge, "tile", outward)
    halo_z = lax.ppermute(halo, "gene", beside)
    other_rows = swap_cores(flat, tiles)
    own_counts, away_counts, own_library = small_counts(scalars, counts)
    other_library = swap_cores(own_library, tiles)
    other_counts = swap_cores(away_counts, tiles)

    gathered = []
    if planned:
        for b, part in enumerate(turn_weights(scalars, weights, came)):
            got = {p: exchanged(part, p, tiles) for p in (1, 2)}
            source, way = {"direct": (part, 3), "x": (got[1], 2), "y": (got[2], 1)}[ROUTES[b]]
            gathered.append([part, got[1], got[2], exchanged(source, way, tiles)])
    else:
        full = lax.all_gather(weights, "tile", axis=0, tiled=True)
        mine = lax.dynamic_slice_in_dim(full, core * core_genes, core_genes, 1)
        gathered = [[part] for part in mine.reshape(-1, LANES, core_blocks, LANES).transpose(2, 0, 3, 1)]

    library = jnp.concatenate([own_library, other_library], axis=0)
    if gene_parts <= 4:
        around = [
            lax.ppermute(library, "gene", [(g, (g + i) % gene_parts) for g in range(gene_parts)])
            for i in range(1, gene_parts)
        ]
        libraries = jnp.stack([library] + around)
    else:
        libraries = lax.psum(library, "gene")[None]
    halos = (halo, halo_z, swap_cores(halo, tiles), swap_cores(halo_z, tiles))

    sources = tuple(
        tuple(pltpu.with_memory_space_constraint(x, pltpu.HBM) for x in group)
        for group in ((flat, other_rows), halos, (own_counts, other_counts))
    )
    *held, factors = load_block(scalars, selection, *sources, libraries, 0, row_count, col_count, gene_total)
    gradients = []
    for b, w_parts in enumerate(gathered):
        following = b + 1 if b + 1 < core_blocks else None
        results = block_gradient(
            scalars, selection, (*held, factors), *sources, w_parts, following, row_count, col_count
        )
        gradients.append(results[: len(w_parts)])
        held = results[len(w_parts) :]
    if not planned:
        part = jnp.stack([part for part, in gradients])
        part = part.transpose(1, 3, 0, 2).reshape(-1, core_genes).astype(jnp.float32)
        nothing = jnp.zeros_like(part)
        low, high = jnp.where(core == 0, part, nothing), jnp.where(core == 0, nothing, part)
        total = lax.psum_scatter(jnp.concatenate([low, high], axis=1), "tile", scatter_dimension=0, tiled=True)
        return total * norm_scale

    arrived = []
    for own, *others in gradients:
        arrived.append([own] + [exchanged(others[p - 1], p, tiles) for p in (1, 2, 3)])
    parts = []
    for pieces in arrived:
        mine, other = summed(scalars, pieces, share, norm_scale)
        parts += [mine, swap_cores(other, tiles)]
    out = placed(scalars, parts[:-2], 0, None, share, local_genes)
    return placed(scalars, parts[-2:], core_blocks - 1, out, share, local_genes)


def solution(mesh):
    in_specs = (P("tile", None, None), P("tile", None, "gene"), P("gene", None), P("tile", "gene"))
    out_specs = P("tile", "gene")

    return jax.shard_map(per_device, mesh=mesh, in_specs=in_specs, out_specs=out_specs, check_vma=False)
```

time: 711 us -> 165 us (0.23)
  waiting for transfers between devices: 241 us -> 19.6 us
  matrix products: 197 us -> 0 us
  local copies, waits for them, and re-layouts: 189 us -> 3.49 us
  Pallas kernels: 0 us -> 83.3 us
  starting transfers between devices: 3.78 us -> 56.2 us
  between operations: 34.1 us -> 0.52 us
  other arithmetic: 29.8 us -> 1.39 us
  blocking collectives: 12.7 us -> 0 us
    psum x1 -> x0, waiting for transfers between devices: 240 us -> none  [per_device(): summed = lax.psum(jnp.concatenate(products, axis=1), 'tile')]
    dot_general x16 -> x0, matrix products: 197 us -> none  [the longest x8 113 us: per_device(): jnp.dot(columns, full_weights[:, 128 * gene_slot:128 * (gene_slot + 1)],...]
    unnamed x86 -> x43, local copies, waits for them, and re-layouts: 165 us -> 2.47 us
    pallas_call x0 -> x13, Pallas kernels: none -> 83.3 us  [the longest x4 54 us: block_gradient(): pl.pallas_call(functools.partial(grad_kernel, plan), in_specs=[SMEM] * 2...]
    ppermute x2 -> x39, starting transfers between devices: 3.74 us -> 56.2 us  [the longest x24 31.1 us: exchanged(): return lax.ppermute(x, 'tile', [(t, t ^ 2 * piece) for t in range(count)])]
    ppermute x2 -> x39, waiting for transfers between devices: 0.01 us -> 19.6 us  [the longest x24 14.3 us: exchanged(): return lax.ppermute(x, 'tile', [(t, t ^ 2 * piece) for t in range(count)])]
    convert_element_type x2 -> x0, other arithmetic: 16.7 us -> none  [the longest x1 8.59 us: per_device(): partial_library = jnp.sum(counts.astype(jnp.float32), axis=2)]
    psum x1 -> x0, blocking collectives: 12.7 us -> none  [per_device(): library = lax.psum(partial_library, 'gene') + 1.0]
  transfers between devices with their start and end apart: 4 -> 39, of which waited for: 1 -> 6; matrix products, arithmetic and copies ran while one was open for 29% -> 2% of each run, Pallas kernels for 0% -> 49%
where the time goes in v1:
time: 165 us; the launch traced here: 164 us
  Pallas kernels  83.3 us (50%)
  starting transfers between devices  56.2 us (34%)
  waiting for transfers between devices  19.6 us (12%)
  local copies, waits for them, and re-layouts  3.49 us (2%)
    pallas_call x4, Pallas kernels, block_gradient(): pl.pallas_call(functools.partial(grad_kernel, plan), in_specs=[SMEM] * 2...  54 us
    ppermute x24, starting transfers between devices, exchanged(): return lax.ppermute(x, 'tile', [(t, t ^ 2 * piece) for t in range(count)])  31.1 us
    ppermute x10, starting transfers between devices, swap_cores(): return lax.ppermute(x, 'tile', [(t, t ^ 1) for t in range(count)])  15 us
    ppermute x24, waiting for transfers between devices, exchanged(): return lax.ppermute(x, 'tile', [(t, t ^ 2 * piece) for t in range(count)])  14.3 us
    pallas_call x4, Pallas kernels, summed(): pl.pallas_call(functools.partial(sum_kernel, scale), in_specs=[SMEM] + [V...  9.33 us
    pallas_call x1, Pallas kernels, small_counts(): pl.pallas_call(counts_kernel, grid_spec=pltpu.PrefetchScalarGridSpec(num_...  8.48 us
    ppermute x3, starting transfers between devices, per_device(): lax.ppermute(library, 'gene', [(g, (g + i) % gene_parts) for g in range(g...  6.84 us
    pallas_call x2, Pallas kernels, placed(): pl.pallas_call(functools.partial(place_kernel, base, len(held)), in_specs...  4.57 us
  transfers between devices with their start and end apart: 39, of which 6 were waited for; matrix products, arithmetic and copies ran while one was open for 2% of the time, Pallas kernels for 49%

profile of v1, /device:TPU:0, one launch (start us, length us, event | category | flops | bytes accessed | tf_op | source)
XLA Modules:
  0.0 164.5 jit_solution(9920680213932498992)
XLA Ops:
  1.1 8.5 %small_counts.1 = (bf16[2048,512]{1,0:T(8,128)(2,1)}, bf16[2048,512]{1,0:T(8,128)(2,1)}, f32[1,2048]{1,0:T(1,128)}) custom-call(s32[3]{0:T(128)} %pad_add_fusion.scalars, s32[8,256,1024]{2,1,0:T(8,128)} %counts_ref.1), custom_call_target="tpu_custom_call" | custom-call | bytes 12582912 | tf_op jit(solution)/shard_map/small_counts/pallas_call | solution.py:56
  11.9 2.6 %collective-permute-start.2 = (bf16[256,768]{1,0:T(8,128)(2,1)S(1)}, bf16[256,768]{1,0:T(8,128)(2,1)S(1)}, u32[]{:S(2)}, u32[]{:S(2)}) collective-permute-start(bf16[256,768]{1,0:T(8,128)(2,1)S(1)} %collective-permute-done.1.rest_2_), channel_id=1, source_target_pairs={{0,1},{1,0},{2,3},{3,2},{4,5},{5,4},{6,7},{7,6},{8,9},{9,8},{10,11... | collective-permute-start | bytes 1179656 | tf_op jit(solution)/shard_map/ppermute | solution.py:395
  14.5 12.5 %collective-permute-start.6 = (f32[1,2048]{1,0:T(1,128)}, f32[1,2048]{1,0:T(1,128)S(1)}, u32[]{:S(2)}, u32[]{:S(2)}) collective-permute-start(f32[1,2048]{1,0:T(1,128)} %get-tuple-element.47), channel_id=1, source_target_pairs={{0,4},{4,0},{8,12},{12,8},{16,20},{20,16},{24,28},{28,24},{1,5},{5... | collective-permute-start | bytes 24584 | tf_op jit(solution)/shard_map/ppermute | solution.py:26
  28.7 2.5 %collective-permute-start.9 = (f32[2,2048]{1,0:T(2,128)S(1)}, f32[2,2048]{1,0:T(2,128)S(1)}, u32[]{:S(2)}, u32[]{:S(2)}) collective-permute-start(f32[2,2048]{1,0:T(2,128)S(1)} %get-tuple-element.86), channel_id=1, source_target_pairs={{0,3},{1,0},{2,1},{3,2},{4,7},{5,4},{6,5},{7,6},{8,11},{9,8},{10,9... | collective-permute-start | bytes 49160 | tf_op jit(solution)/shard_map/ppermute | solution.py:415
  32.7 2.6 %collective-permute-start.8 = (f32[2,2048]{1,0:T(2,128)S(1)}, f32[2,2048]{1,0:T(2,128)S(1)}, u32[]{:S(2)}, u32[]{:S(2)}) collective-permute-start(f32[2,2048]{1,0:T(2,128)S(1)} %get-tuple-element.86), channel_id=1, source_target_pairs={{0,2},{1,3},{2,0},{3,1},{4,6},{5,7},{6,4},{7,5},{8,10},{9,11},{10,... | collective-permute-start | bytes 49160 | tf_op jit(solution)/shard_map/ppermute | solution.py:415
  35.3 2.1 %collective-permute-done.8 = f32[2,2048]{1,0:T(2,128)S(1)} collective-permute-done((f32[2,2048]{1,0:T(2,128)S(1)}, f32[2,2048]{1,0:T(2,128)S(1)}, u32[]{:S(2)}, u32[]{:S(2)}) %collective-permute-start.8) | collective-permute-done | bytes 16416 | tf_op jit(solution)/shard_map/ppermute | solution.py:415
  39.6 3.4 %turn_weights.1 = (bf16[9,128,128]{2,1,0:T(8,128)(2,1)}, bf16[9,128,128]{2,1,0:T(8,128)(2,1)}, bf16[9,128,128]{2,1,0:T(8,128)(2,1)}, bf16[9,128,128]{2,1,0:T(8,128)(2,1)}) custom-call(s32[3]{0:T(128)} %pad_add_fusion.scalars, bf16[576,1024]{1,0:T(8,128)(2,1)} %mine_ref.1, bf16[576,1024]{1,0:T(8,128)(2,1)} %collective-permute-done.10.came_ref), custom_call_target="tpu_custom_call" | custom-call | bytes 3538944 | tf_op jit(solution)/shard_map/turn_weights/pallas_call | solution.py:89
  43.7 3.1 %collective-permute-start.11 = (bf16[9,128,128]{2,1,0:T(8,128)(2,1)}, bf16[9,128,128]{2,1,0:T(8,128)(2,1)S(1)}, u32[]{:S(2)}, u32[]{:S(2)}) collective-permute-start(bf16[9,128,128]{2,1,0:T(8,128)(2,1)} %get-tuple-element.51.rest_8_), channel_id=1, source_target_pairs={{0,8},{4,12},{8,0},{12,4},{16,24},{20,28},{24,16},{28,20},{1,9},{5... | collective-permute-start | bytes 884744 | tf_op jit(solution)/shard_map/ppermute | solution.py:367
  51.4 3.6 %load_block.1 = (bf16[4608,512]{1,0:T(8,128)(2,1)S(1)}, bf16[4096,128]{1,0:T(8,128)(2,1)S(1)}, f32[1,4096]{1,0:T(1,128)S(1)}) custom-call(s32[3]{0:T(128)S(1)} %copy-done, s32[8,4]{1,0:T(8,128)S(1)} %copy.7.selection, bf16[2048,1536]{1,0:T(8,128)(2,1)} %bitcast.12, bf16[2048,1536]{1,0:T(8,128)(2,1)} %collective-permute-done.rest_1_, ...), custom_call_target="tpu_custom_call" | custom-call | bytes 12582912 | tf_op jit(solution)/shard_map/load_block/pallas_call | solution.py:177
  55.0 2.1 %collective-permute-start.20 = (bf16[9,128,128]{2,1,0:T(8,128)(2,1)S(1)}, bf16[9,128,128]{2,1,0:T(8,128)(2,1)S(1)}, u32[]{:S(2)}, u32[]{:S(2)}) collective-permute-start(bf16[9,128,128]{2,1,0:T(8,128)(2,1)S(1)} %copy-done.3), channel_id=1, source_target_pairs={{0,24},{4,28},{8,16},{12,20},{16,8},{20,12},{24,0},{28,4},{1,25},{... | collective-permute-start | bytes 884744 | tf_op jit(solution)/shard_map/ppermute | solution.py:367
  57.1 5.8 %collective-permute-done.12.rest_10_ = bf16[9,128,128]{2,1,0:T(8,128)(2,1)S(1)} collective-permute-done((bf16[9,128,128]{2,1,0:T(8,128)(2,1)}, bf16[9,128,128]{2,1,0:T(8,128)(2,1)S(1)}, u32[]{:S(2)}, u32[]{:S(2)}) %collective-permute-start.12) | collective-permute-done | bytes 294944 | tf_op jit(solution)/shard_map/ppermute | solution.py:367
  64.0 2.0 %collective-permute-start.33 = (bf16[9,128,128]{2,1,0:T(8,128)(2,1)S(1)}, bf16[9,128,128]{2,1,0:T(8,128)(2,1)S(1)}, u32[]{:S(2)}, u32[]{:S(2)}) collective-permute-start(bf16[9,128,128]{2,1,0:T(8,128)(2,1)S(1)} %copy-done.1), channel_id=1, source_target_pairs={{0,16},{4,20},{8,24},{12,28},{16,0},{20,4},{24,8},{28,12},{1,17},{... | collective-permute-start | bytes 884744 | tf_op jit(solution)/shard_map/ppermute | solution.py:367
  66.0 13.4 %block_gradient.4 = (bf16[9,128,128]{2,1,0:T(8,128)(2,1)}, bf16[9,128,128]{2,1,0:T(8,128)(2,1)}, bf16[9,128,128]{2,1,0:T(8,128)(2,1)}, bf16[9,128,128]{2,1,0:T(8...) custom-call(s32[3]{0:T(128)S(1)} %copy-done, s32[8,4]{1,0:T(8,128)S(1)} %copy.7.selection, ...), custom_call_target="tpu_custom_call" | custom-call | flops 9663676416 | bytes 10485760 | tf_op jit(solution)/shard_map/block_gradient/pallas_call | solution.py:285
  80.5 2.6 %collective-permute-start.27 = (bf16[9,128,128]{2,1,0:T(8,128)(2,1)S(1)}, bf16[9,128,128]{2,1,0:T(8,128)(2,1)S(1)}, u32[]{:S(2)}, u32[]{:S(2)}) collective-permute-start(bf16[9,128,128]{2,1,0:T(8,128)(2,1)S(1)} %collective-permute-done.25.rest_9_), channel_id=1, source_target_pairs={{0,16},{4,20},{8,24},{12,28},{16,0},{20,4},{24,8},{28,12},{1,17},{... | collective-permute-start | bytes 884744 | tf_op jit(solution)/shard_map/ppermute | solution.py:367
  85.1 13.6 %block_gradient.5 = (bf16[9,128,128]{2,1,0:T(8,128)(2,1)}, bf16[9,128,128]{2,1,0:T(8,128)(2,1)}, bf16[9,128,128]{2,1,0:T(8,128)(2,1)}, bf16[9,128,128]{2,1,0:T(8...) custom-call(s32[3]{0:T(128)S(1)} %copy-done, s32[8,4]{1,0:T(8,128)S(1)} %copy.7.selection, ...), custom_call_target="tpu_custom_call" | custom-call | flops 9663676416 | bytes 10485760 | tf_op jit(solution)/shard_map/block_gradient/pallas_call | solution.py:285
  98.8 2.0 %collective-permute-start.16 = (bf16[9,128,128]{2,1,0:T(8,128)(2,1)S(1)}, bf16[9,128,128]{2,1,0:T(8,128)(2,1)S(1)}, u32[]{:S(2)}, u32[]{:S(2)}) collective-permute-start(bf16[9,128,128]{2,1,0:T(8,128)(2,1)S(1)} %copy-done.16), channel_id=1, source_target_pairs={{0,24},{4,28},{8,16},{12,20},{16,8},{20,12},{24,0},{28,4},{1,25},{... | collective-permute-start | bytes 884744 | tf_op jit(solution)/shard_map/ppermute | solution.py:367
  100.8 13.6 %block_gradient.6 = (bf16[9,128,128]{2,1,0:T(8,128)(2,1)}, bf16[9,128,128]{2,1,0:T(8,128)(2,1)}, bf16[9,128,128]{2,1,0:T(8,128)(2,1)}, bf16[9,128,128]{2,1,0:T(8...) custom-call(s32[3]{0:T(128)S(1)} %copy-done, s32[8,4]{1,0:T(8,128)S(1)} %copy.7.selection, ...), custom_call_target="tpu_custom_call" | custom-call | flops 9663676416 | bytes 10485760 | tf_op jit(solution)/shard_map/block_gradient/pallas_call | solution.py:285
  119.5 13.4 %block_gradient.7 = (bf16[9,128,128]{2,1,0:T(8,128)(2,1)}, bf16[9,128,128]{2,1,0:T(8,128)(2,1)}, bf16[9,128,128]{2,1,0:T(8,128)(2,1)}, bf16[9,128,128]{2,1,0:T(8,128)(2,1)}) custom-call(s32[3]{0:T(128)S(1)} %copy-done, s32[8,4]{1,0:T(8,128)S(1)} %copy.7.selection, bf16[4608,512]{1,0:T(8,128)(2,1)S(1)} %get-tuple-element.76.fs, ...), custom_call_target="tpu_custom_call" | custom-call | flops 9663676416 | bytes 10485760 | tf_op jit(solution)/shard_map/block_gradient/pallas_call | solution.py:285
  138.5 2.3 %summed.4 = (f32[576,128]{1,0:T(8,128)}, f32[576,128]{1,0:T(8,128)}) custom-call(s32[3]{0:T(128)} %pad_add_fusion.scalars, bf16[9,128,128]{2,1,0:T(8,128)(2,1)} %get-tuple-element.52.rest_0_, bf16[9,128,128]{2,1,0:T(8,128)(2,1)} %copy-done.10, bf16[9,128,128]{2,1,0:T(8,128)(2,1)} %copy-done.11, bf16[9,128,128]{2,1,0:T(8,128)(2,1)} %copy-done.12), custom_call_target="tpu_custom_call" | custom-call | bytes 589824 | tf_op jit(solution)/shard_map/summed/pallas_call | solution.py:324
  140.9 2.3 %summed.5 = (f32[576,128]{1,0:T(8,128)}, f32[576,128]{1,0:T(8,128)}) custom-call(s32[3]{0:T(128)} %pad_add_fusion.scalars, bf16[9,128,128]{2,1,0:T(8,128)(2,1)} %get-tuple-element.61.rest_0_, bf16[9,128,128]{2,1,0:T(8,128)(2,1)} %collective-permute-done.21.rest_1_, bf16[9,128,128]{2,1,0:T(8,128)(2,1)} %collective-permute-done.22.rest_2_, ...), custom_call_target="tpu_custom_call" | custom-call | bytes 589824 | tf_op jit(solution)/shard_map/summed/pallas_call | solution.py:324
  143.2 8.5 %collective-permute-done.29.rest_2_ = bf16[9,128,128]{2,1,0:T(8,128)(2,1)S(1)} collective-permute-done((bf16[9,128,128]{2,1,0:T(8,128)(2,1)}, bf16[9,128,128]{2,1,0:T(8,128)(2,1)S(1)}, u32[]{:S(2)}, u32[]{:S(2)}) %collective-permute-start.29) | collective-permute-done | bytes 294944 | tf_op jit(solution)/shard_map/ppermute | solution.py:367
  153.6 2.3 %summed.6 = (f32[576,128]{1,0:T(8,128)}, f32[576,128]{1,0:T(8,128)}) custom-call(s32[3]{0:T(128)} %pad_add_fusion.scalars, bf16[9,128,128]{2,1,0:T(8,128)(2,1)} %get-tuple-element.70.rest_0_, bf16[9,128,128]{2,1,0:T(8,128)(2,1)} %collective-permute-done.28.rest_1_, bf16[9,128,128]{2,1,0:T(8,128)(2,1)} %copy-done.13, bf16[9,128,128]{2,1,0:T(8,128)(2,1)} %copy-done.14), custom_call_target="tpu_custom_call" | custom-call | bytes 589824 | tf_op jit(solution)/shard_map/summed/pallas_call | solution.py:324
  155.9 2.3 %summed.7 = (f32[576,128]{1,0:T(8,128)}, f32[576,128]{1,0:T(8,128)}) custom-call(s32[3]{0:T(128)} %pad_add_fusion.scalars, bf16[9,128,128]{2,1,0:T(8,128)(2,1)} %get-tuple-element.79.rest_0_, bf16[9,128,128]{2,1,0:T(8,128)(2,1)} %collective-permute-done.35.rest_1_, bf16[9,128,128]{2,1,0:T(8,128)(2,1)} %collective-permute-done.36.rest_2_, ...), custom_call_target="tpu_custom_call" | custom-call | bytes 589824 | tf_op jit(solution)/shard_map/summed/pallas_call | solution.py:324
  159.7 2.7 %placed.2.rest_0_ = f32[576,1024]{1,0:T(8,128)} custom-call(s32[3]{0:T(128)} %pad_add_fusion.scalars, f32[576,128]{1,0:T(8,128)} %get-tuple-element.56.rest_0_, f32[576,128]{1,0:T(8,128)} %copy-done.7, f32[576,128]{1,0:T(8,128)} %get-tuple-element.65.rest_2_, f32[576,128]{1,0:T(8,128)} %copy-done.8, f32[576,128]{1,0:T(8,128)} %get-tuple-element.74.rest_4_, ...), custom_call_target="tpu_custom_call" | custom-call | bytes 3538944 | tf_op jit(solution)/shard_map/placed/pallas_call | solution.py:353
  (114 shorter events, 34.3 us)
Async XLA Ops:
  0.0 50.5 %collective-permute-start = (bf16[2048,1536]{1,0:T(8,128)(2,1)}, bf16[2048,1536]{1,0:T(8,128)(2,1)}, u32[]{:S(2)}, u32[]{:S(2)}) collective-permute-start(bf16[2048,1536]{1,0:T(8,128)(2,1)} %bitcast.11), channel_id=1, source_target_pairs={{0,4},{4,0},{8,12},{12,8},{16,20},{20,16},{24,28},{28,24},{1,5},{5... | collective-permute-start | bytes 18874376 | tf_op jit(solution)/shard_map/ppermute | solution.py:26
  9.6 39.6 %collective-permute-start.5 = (bf16[2048,512]{1,0:T(8,128)(2,1)}, bf16[2048,512]{1,0:T(8,128)(2,1)}, u32[]{:S(2)}, u32[]{:S(2)}) collective-permute-start(bf16[2048,512]{1,0:T(8,128)(2,1)} %get-tuple-element.46), channel_id=1, source_target_pairs={{0,4},{4,0},{8,12},{12,8},{16,20},{20,16},{24,28},{28,24},{1,5},{5... | collective-permute-start | bytes 6291464 | tf_op jit(solution)/shard_map/ppermute | solution.py:26
  9.6 28.2 %collective-permute-start.10 = (bf16[576,1024]{1,0:T(8,128)(2,1)}, bf16[576,1024]{1,0:T(8,128)(2,1)}, u32[]{:S(2)}, u32[]{:S(2)}) collective-permute-start(bf16[576,1024]{1,0:T(8,128)(2,1)} %mine_ref.1), channel_id=1, source_target_pairs={{0,4},{4,0},{8,12},{12,8},{16,20},{20,16},{24,28},{28,24},{1,5},{5... | collective-permute-start | bytes 3538952 | tf_op jit(solution)/shard_map/ppermute | solution.py:26
  11.9 25.5 %collective-permute-start.2 = (bf16[256,768]{1,0:T(8,128)(2,1)S(1)}, bf16[256,768]{1,0:T(8,128)(2,1)S(1)}, u32[]{:S(2)}, u32[]{:S(2)}) collective-permute-start(bf16[256,768]{1,0:T(8,128)(2,1)S(1)} %collective-permute-done.1.rest_2_), channel_id=1, source_target_pairs={{0,1},{1,0},{2,3},{3,2},{4,5},{5,4},{6,7},{7,6},{8,9},{9,8},{10,11... | collective-permute-start | bytes 1179656 | tf_op jit(solution)/shard_map/ppermute | solution.py:395
  49.2 30.2 %collective-permute-start.18 = (bf16[9,128,128]{2,1,0:T(8,128)(2,1)}, bf16[9,128,128]{2,1,0:T(8,128)(2,1)S(1)}, u32[]{:S(2)}, u32[]{:S(2)}) collective-permute-start(bf16[9,128,128]{2,1,0:T(8,128)(2,1)} %get-tuple-element.60.rest_8_), channel_id=1, source_target_pairs={{0,8},{4,12},{8,0},{12,4},{16,24},{20,28},{24,16},{28,20},{1,9},{5... | collective-permute-start | bytes 884744 | tf_op jit(solution)/shard_map/ppermute | solution.py:367
  50.5 29.1 %collective-permute-start.19 = (bf16[9,128,128]{2,1,0:T(8,128)(2,1)}, bf16[9,128,128]{2,1,0:T(8,128)(2,1)S(1)}, u32[]{:S(2)}, u32[]{:S(2)}) collective-permute-start(bf16[9,128,128]{2,1,0:T(8,128)(2,1)} %get-tuple-element.60.rest_8_), channel_id=1, source_target_pairs={{0,16},{4,20},{8,24},{12,28},{16,0},{20,4},{24,8},{28,12},{1,17},{... | collective-permute-start | bytes 884744 | tf_op jit(solution)/shard_map/ppermute | solution.py:367
  55.0 28.6 %collective-permute-start.20 = (bf16[9,128,128]{2,1,0:T(8,128)(2,1)S(1)}, bf16[9,128,128]{2,1,0:T(8,128)(2,1)S(1)}, u32[]{:S(2)}, u32[]{:S(2)}) collective-permute-start(bf16[9,128,128]{2,1,0:T(8,128)(2,1)S(1)} %copy-done.3), channel_id=1, source_target_pairs={{0,24},{4,28},{8,16},{12,20},{16,8},{20,12},{24,0},{28,4},{1,25},{... | collective-permute-start | bytes 884744 | tf_op jit(solution)/shard_map/ppermute | solution.py:367
  64.0 19.0 %collective-permute-start.33 = (bf16[9,128,128]{2,1,0:T(8,128)(2,1)S(1)}, bf16[9,128,128]{2,1,0:T(8,128)(2,1)S(1)}, u32[]{:S(2)}, u32[]{:S(2)}) collective-permute-start(bf16[9,128,128]{2,1,0:T(8,128)(2,1)S(1)} %copy-done.1), channel_id=1, source_target_pairs={{0,16},{4,20},{8,24},{12,28},{16,0},{20,4},{24,8},{28,12},{1,17},{... | collective-permute-start | bytes 884744 | tf_op jit(solution)/shard_map/ppermute | solution.py:367
  79.4 19.2 %collective-permute-start.26 = (bf16[9,128,128]{2,1,0:T(8,128)(2,1)S(1)}, bf16[9,128,128]{2,1,0:T(8,128)(2,1)S(1)}, u32[]{:S(2)}, u32[]{:S(2)}) collective-permute-start(bf16[9,128,128]{2,1,0:T(8,128)(2,1)S(1)} %copy-done.2), channel_id=1, source_target_pairs={{0,16},{4,20},{8,24},{12,28},{16,0},{20,4},{24,8},{28,12},{1,17},{... | collective-permute-start | bytes 884744 | tf_op jit(solution)/shard_map/ppermute | solution.py:367
  79.6 34.8 %collective-permute-start.32 = (bf16[9,128,128]{2,1,0:T(8,128)(2,1)S(1)}, bf16[9,128,128]{2,1,0:T(8,128)(2,1)S(1)}, u32[]{:S(2)}, u32[]{:S(2)}) collective-permute-start(bf16[9,128,128]{2,1,0:T(8,128)(2,1)S(1)} %copy-done.1), channel_id=1, source_target_pairs={{0,8},{4,12},{8,0},{12,4},{16,24},{20,28},{24,16},{28,20},{1,9},{5... | collective-permute-start | bytes 884744 | tf_op jit(solution)/shard_map/ppermute | solution.py:367
  80.5 18.3 %collective-permute-start.27 = (bf16[9,128,128]{2,1,0:T(8,128)(2,1)S(1)}, bf16[9,128,128]{2,1,0:T(8,128)(2,1)S(1)}, u32[]{:S(2)}, u32[]{:S(2)}) collective-permute-start(bf16[9,128,128]{2,1,0:T(8,128)(2,1)S(1)} %collective-permute-done.25.rest_9_), channel_id=1, source_target_pairs={{0,16},{4,20},{8,24},{12,28},{16,0},{20,4},{24,8},{28,12},{1,17},{... | collective-permute-start | bytes 884744 | tf_op jit(solution)/shard_map/ppermute | solution.py:367
  83.0 32.9 %collective-permute-start.34 = (bf16[9,128,128]{2,1,0:T(8,128)(2,1)S(1)}, bf16[9,128,128]{2,1,0:T(8,128)(2,1)S(1)}, u32[]{:S(2)}, u32[]{:S(2)}) collective-permute-start(bf16[9,128,128]{2,1,0:T(8,128)(2,1)S(1)} %collective-permute-done.33.rest_10_), channel_id=1, source_target_pairs={{0,8},{4,12},{8,0},{12,4},{16,24},{20,28},{24,16},{28,20},{1,9},{5... | collective-permute-start | bytes 884744 | tf_op jit(solution)/shard_map/ppermute | solution.py:367
  83.6 32.5 %collective-permute-start.14 = (bf16[9,128,128]{2,1,0:T(8,128)(2,1)}, bf16[9,128,128]{2,1,0:T(8,128)(2,1)S(1)}, u32[]{:S(2)}, u32[]{:S(2)}) collective-permute-start(bf16[9,128,128]{2,1,0:T(8,128)(2,1)} %get-tuple-element.53), channel_id=1, source_target_pairs={{0,8},{4,12},{8,0},{12,4},{16,24},{20,28},{24,16},{28,20},{1,9},{5... | collective-permute-start | bytes 884744 | tf_op jit(solution)/shard_map/ppermute | solution.py:367
  98.7 19.4 %collective-permute-start.15 = (bf16[9,128,128]{2,1,0:T(8,128)(2,1)S(1)}, bf16[9,128,128]{2,1,0:T(8,128)(2,1)S(1)}, u32[]{:S(2)}, u32[]{:S(2)}) collective-permute-start(bf16[9,128,128]{2,1,0:T(8,128)(2,1)S(1)} %copy-done.18), channel_id=1, source_target_pairs={{0,16},{4,20},{8,24},{12,28},{16,0},{20,4},{24,8},{28,12},{1,17},{... | collective-permute-start | bytes 884744 | tf_op jit(solution)/shard_map/ppermute | solution.py:367
  98.8 34.1 %collective-permute-start.16 = (bf16[9,128,128]{2,1,0:T(8,128)(2,1)S(1)}, bf16[9,128,128]{2,1,0:T(8,128)(2,1)S(1)}, u32[]{:S(2)}, u32[]{:S(2)}) collective-permute-start(bf16[9,128,128]{2,1,0:T(8,128)(2,1)S(1)} %copy-done.16), channel_id=1, source_target_pairs={{0,24},{4,28},{8,16},{12,20},{16,8},{20,12},{24,0},{28,4},{1,25},{... | collective-permute-start | bytes 884744 | tf_op jit(solution)/shard_map/ppermute | solution.py:367
  114.4 18.7 %collective-permute-start.21 = (bf16[9,128,128]{2,1,0:T(8,128)(2,1)S(1)}, bf16[9,128,128]{2,1,0:T(8,128)(2,1)}, u32[]{:S(2)}, u32[]{:S(2)}) collective-permute-start(bf16[9,128,128]{2,1,0:T(8,128)(2,1)S(1)} %copy-done.20), channel_id=1, source_target_pairs={{0,8},{4,12},{8,0},{12,4},{16,24},{20,28},{24,16},{28,20},{1,9},{5... | collective-permute-start | bytes 884744 | tf_op jit(solution)/shard_map/ppermute | solution.py:367
  115.9 19.1 %collective-permute-start.22 = (bf16[9,128,128]{2,1,0:T(8,128)(2,1)S(1)}, bf16[9,128,128]{2,1,0:T(8,128)(2,1)}, u32[]{:S(2)}, u32[]{:S(2)}) collective-permute-start(bf16[9,128,128]{2,1,0:T(8,128)(2,1)S(1)} %copy-done.19), channel_id=1, source_target_pairs={{0,16},{4,20},{8,24},{12,28},{16,0},{20,4},{24,8},{28,12},{1,17},{... | collective-permute-start | bytes 884744 | tf_op jit(solution)/shard_map/ppermute | solution.py:367
  116.1 20.4 %collective-permute-start.23 = (bf16[9,128,128]{2,1,0:T(8,128)(2,1)S(1)}, bf16[9,128,128]{2,1,0:T(8,128)(2,1)}, u32[]{:S(2)}, u32[]{:S(2)}) collective-permute-start(bf16[9,128,128]{2,1,0:T(8,128)(2,1)S(1)} %copy-done.17), channel_id=1, source_target_pairs={{0,24},{4,28},{8,16},{12,20},{16,8},{20,12},{24,0},{28,4},{1,25},{... | collective-permute-start | bytes 884744 | tf_op jit(solution)/shard_map/ppermute | solution.py:367
  118.0 18.6 %collective-permute-start.28 = (bf16[9,128,128]{2,1,0:T(8,128)(2,1)}, bf16[9,128,128]{2,1,0:T(8,128)(2,1)}, u32[]{:S(2)}, u32[]{:S(2)}) collective-permute-start(bf16[9,128,128]{2,1,0:T(8,128)(2,1)} %get-tuple-element.71), channel_id=1, source_target_pairs={{0,8},{4,12},{8,0},{12,4},{16,24},{20,28},{24,16},{28,20},{1,9},{5... | collective-permute-start | bytes 884744 | tf_op jit(solution)/shard_map/ppermute | solution.py:367
  132.9 18.7 %collective-permute-start.29 = (bf16[9,128,128]{2,1,0:T(8,128)(2,1)}, bf16[9,128,128]{2,1,0:T(8,128)(2,1)S(1)}, u32[]{:S(2)}, u32[]{:S(2)}) collective-permute-start(bf16[9,128,128]{2,1,0:T(8,128)(2,1)} %get-tuple-element.72), channel_id=1, source_target_pairs={{0,16},{4,20},{8,24},{12,28},{16,0},{20,4},{24,8},{28,12},{1,17},{... | collective-permute-start | bytes 884744 | tf_op jit(solution)/shard_map/ppermute | solution.py:367
  133.1 19.3 %collective-permute-start.30 = (bf16[9,128,128]{2,1,0:T(8,128)(2,1)}, bf16[9,128,128]{2,1,0:T(8,128)(2,1)S(1)}, u32[]{:S(2)}, u32[]{:S(2)}) collective-permute-start(bf16[9,128,128]{2,1,0:T(8,128)(2,1)} %get-tuple-element.73), channel_id=1, source_target_pairs={{0,24},{4,28},{8,16},{12,20},{16,8},{20,12},{24,0},{28,4},{1,25},{... | collective-permute-start | bytes 884744 | tf_op jit(solution)/shard_map/ppermute | solution.py:367
  135.0 20.9 %collective-permute-start.35 = (bf16[9,128,128]{2,1,0:T(8,128)(2,1)}, bf16[9,128,128]{2,1,0:T(8,128)(2,1)}, u32[]{:S(2)}, u32[]{:S(2)}) collective-permute-start(bf16[9,128,128]{2,1,0:T(8,128)(2,1)} %get-tuple-element.80), channel_id=1, source_target_pairs={{0,8},{4,12},{8,0},{12,4},{16,24},{20,28},{24,16},{28,20},{1,9},{5... | collective-permute-start | bytes 884744 | tf_op jit(solution)/shard_map/ppermute | solution.py:367
  136.5 19.4 %collective-permute-start.36 = (bf16[9,128,128]{2,1,0:T(8,128)(2,1)}, bf16[9,128,128]{2,1,0:T(8,128)(2,1)}, u32[]{:S(2)}, u32[]{:S(2)}) collective-permute-start(bf16[9,128,128]{2,1,0:T(8,128)(2,1)} %get-tuple-element.81), channel_id=1, source_target_pairs={{0,16},{4,20},{8,24},{12,28},{16,0},{20,4},{24,8},{28,12},{1,17},{... | collective-permute-start | bytes 884744 | tf_op jit(solution)/shard_map/ppermute | solution.py:367
  136.6 19.3 %collective-permute-start.37 = (bf16[9,128,128]{2,1,0:T(8,128)(2,1)}, bf16[9,128,128]{2,1,0:T(8,128)(2,1)}, u32[]{:S(2)}, u32[]{:S(2)}) collective-permute-start(bf16[9,128,128]{2,1,0:T(8,128)(2,1)} %get-tuple-element.82), channel_id=1, source_target_pairs={{0,24},{4,28},{8,16},{12,20},{16,8},{20,12},{24,0},{28,4},{1,25},{... | collective-permute-start | bytes 884744 | tf_op jit(solution)/shard_map/ppermute | solution.py:367
  (36 other events, 435.5 us)

commit v2 on v1

--- a/solution.py
+++ b/solution.py
@@ -11,7 +11,7 @@
 
 LANES = 128
 STEPS = 3
-ROUTES = ("direct", "direct", "x", "y")
+GROUPS = ((0,), (1,), (2, 3))
 
 NT = (((1,), (1,)), ((), ()))
 KERNEL_VMEM = pltpu.CompilerParams(vmem_limit_bytes=24_000_000)
@@ -20,6 +20,10 @@
 VMEM = pl.BlockSpec(memory_space=pltpu.VMEM)
 SMEM = pl.BlockSpec(memory_space=pltpu.SMEM)
 ANY = pl.BlockSpec(memory_space=pl.ANY)
+
+
+def in_hbm(x):
+    return pltpu.with_memory_space_constraint(x, pltpu.HBM)
 
 
 def swap_cores(x, count):
@@ -76,21 +80,21 @@
     lanes = pl.ds(pl.multiple_of(core * genes, genes), genes)
     rows[pl.ds(pl.multiple_of(core * share, 16), share), :] = mine_ref[:, lanes]
     rows[pl.ds(pl.multiple_of((1 - core) * share, 16), share), :] = came_ref[:, lanes]
-    for j, part in enumerate(parts):
-        for b in range(rows.shape[0] // LANES):
-            block = rows[b * LANES : (b + 1) * LANES, j * LANES : (j + 1) * LANES]
-            part[b] = turned(block).astype(jnp.bfloat16)
+    for part, group in zip(parts, GROUPS):
+        for i, j in enumerate(group):
+            for b in range(rows.shape[0] // LANES):
+                block = rows[b * LANES : (b + 1) * LANES, j * LANES : (j + 1) * LANES]
+                part[i, b] = turned(block).astype(jnp.bfloat16)
 
 
 def turn_weights(scalars, mine, came):
     share, genes = mine.shape
-    blocks = genes // 2 // LANES
-    part = jax.ShapeDtypeStruct((2 * share // LANES, LANES, LANES), jnp.bfloat16)
+    shape = (2 * share // LANES, LANES, LANES)
     return pl.pallas_call(
         weights_kernel,
         in_specs=[SMEM, VMEM, VMEM],
-        out_specs=[VMEM] * blocks,
-        out_shape=[part] * blocks,
+        out_specs=[VMEM] * len(GROUPS),
+        out_shape=[jax.ShapeDtypeStruct((len(group),) + shape, jnp.bfloat16) for group in GROUPS],
         scratch_shapes=[pltpu.VMEM((2 * share, genes // 2), jnp.bfloat16)],
         compiler_params=ALL_VMEM,
         name="turn_weights",
@@ -99,11 +103,10 @@
 
 
 def block_copies(own_rows, cols, block, scalars, selection, features, halos, counts, fs, cs, f_sem, c_sem):
-    core, parity = scalars[0], scalars[2]
+    core = scalars[0]
     own_bins = own_rows * cols
     reads = selection.shape[1]
     row = core * (selection.shape[0] // 2) + block
-    half_blocks = halos[0].shape[1] // LANES
     spans = ((0, cols), (cols, own_bins), (cols + own_bins, own_bins), (cols + 2 * own_bins, cols))
 
     def feature_copy(place, k, source, feature_block):
@@ -123,18 +126,12 @@
         @pl.when(core == this)
         def _():
             near, far = features if this == 0 else features[::-1]
-            top, bottom = (halos[:2], halos[2:]) if this == 0 else (halos[2:], halos[:2])
             for k in range(reads):
                 chosen = selection[row, k]
                 feature_copy(1, k, near, chosen).start()
                 feature_copy(2, k, far, chosen).start()
-                upper = jnp.where(chosen >= half_blocks, 1, 0)
-                for held in range(2):
-
-                    @pl.when((upper == parity) == (held == 0))
-                    def _():
-                        feature_copy(0, k, top[held], chosen - upper * half_blocks).start()
-                        feature_copy(3, k, bottom[held], chosen - upper * half_blocks).start()
+                feature_copy(0, k, halos[this], chosen).start()
+                feature_copy(3, k, halos[1 - this], chosen).start()
 
             for side, source in enumerate(counts if this == 0 else counts[::-1]):
                 count_copy(side, source).start()
@@ -151,15 +148,12 @@
 
 def load_kernel(plan, scalars, selection, *rest):
     own_rows, cols, block, gene_total = plan
-    features, halos, counts, libraries, rest = rest[:2], rest[2:6], rest[6:8], rest[8], rest[9:]
+    features, halos, counts, libraries, rest = rest[:2], rest[2:4], rest[4:6], rest[6:8], rest[8:]
     fs, cs, ls, f_sem, c_sem = rest
     wait = block_copies(own_rows, cols, block, scalars, selection, features, halos, counts, fs, cs, f_sem, c_sem)
     own_bins = own_rows * cols
     core = scalars[0]
-    total = libraries[0]
-    for i in range(1, libraries.shape[0]):
-        total += libraries[i]
-    sizes = (total + 1.0) / gene_total
+    sizes = (libraries[0][...] + libraries[1][...] + 1.0) / gene_total
     ls[:, pl.ds(pl.multiple_of(core * own_bins, own_bins), own_bins)] = sizes[:1]
     ls[:, pl.ds(pl.multiple_of((1 - core) * own_bins, own_bins), own_bins)] = sizes[1:]
     wait()
@@ -176,19 +170,19 @@
     bins, reads = 2 * own_rows * cols, selection.shape[1]
     return pl.pallas_call(
         functools.partial(load_kernel, (own_rows, cols, block, gene_total)),
-        in_specs=[SMEM] * 2 + [HBM] * 8 + [VMEM],
+        in_specs=[SMEM] * 2 + [HBM] * 6 + [VMEM] * 2,
         out_specs=[VMEM] * 3,
         out_shape=loaded(bins, cols, reads) + [pltpu.VMEM((1, bins), jnp.float32)],
         scratch_shapes=[pltpu.SemaphoreType.DMA((4, reads)), pltpu.SemaphoreType.DMA((2,))],
         compiler_params=KERNEL_VMEM,
         name="load_block",
         cost_estimate=pl.CostEstimate(flops=0, bytes_accessed=12 * 2**20, transcendentals=0),
-    )(scalars, selection, *features, *halos, *counts, libraries)
+    )(scalars, selection, *features, *halos, *counts, *libraries)
 
 
 def grad_kernel(plan, scalars, selection, fs, cs, ls, *rest):
-    own_rows, cols, following, pieces, piece_blocks = plan
-    features, halos, counts, rest = rest[:2], rest[2:6], rest[6:8], rest[8:]
+    own_rows, cols, offset, following, pieces, piece_blocks = plan
+    features, halos, counts, rest = rest[:2], rest[2:4], rest[4:6], rest[6:]
     w_parts, g_parts, rest = rest[:pieces], rest[pieces : 2 * pieces], rest[2 * pieces :]
     wait_next = None
     if following is not None:
@@ -201,21 +195,22 @@
         return (scalars[1] ^ p) * piece_blocks if pieces > 1 else 0
 
     weight_copies = [
-        pltpu.make_async_copy(w_parts[p], wv.at[pl.ds(first_block(p), piece_blocks)], w_sem.at[p])
+        pltpu.make_async_copy(w_parts[p].at[offset], wv.at[pl.ds(first_block(p), piece_blocks)], w_sem.at[p])
         for p in range(pieces)
     ]
     for copy in weight_copies:
         copy.start()
-    if following is not None:
-        wait_next = block_copies(
-            own_rows, cols, following, scalars, selection, features, halos, counts, next_fs, next_cs, f_sem, c_sem
-        )
     for copy in weight_copies:
         copy.wait()
     for d in range(STEPS):
         for e in range(STEPS):
             for k in range(reads):
                 wl[d, e * LANES : (e + 1) * LANES, k * LANES : (k + 1) * LANES] = wv[(STEPS * d + e) * reads + k]
+
+    if following is not None:
+        wait_next = block_copies(
+            own_rows, cols, following, scalars, selection, features, halos, counts, next_fs, next_cs, f_sem, c_sem
+        )
 
     lane = lax.broadcasted_iota(jnp.int32, (LANES, cols), 1)
 
@@ -272,19 +267,19 @@
         copy.wait()
 
 
-def block_gradient(scalars, selection, held, features, halos, counts, w_parts, following, own_rows, cols):
+def block_gradient(scalars, selection, held, features, halos, counts, w_parts, offset, following, own_rows, cols):
     pieces = len(w_parts)
-    piece_blocks = w_parts[0].shape[0]
+    piece_blocks = w_parts[0].shape[1]
     reads = selection.shape[1]
     rows = 2 * own_rows
     taps = STEPS * STEPS * reads
     bins = rows * cols
-    plan = (own_rows, cols, following, pieces, piece_blocks)
+    plan = (own_rows, cols, offset, following, pieces, piece_blocks)
     more = [] if following is None else loaded(bins, cols, reads)
     part = pltpu.HBM((piece_blocks, LANES, LANES), jnp.bfloat16)
     return pl.pallas_call(
         functools.partial(grad_kernel, plan),
-        in_specs=[SMEM] * 2 + [VMEM] * 3 + [HBM] * 8 + [ANY] * pieces,
+        in_specs=[SMEM] * 2 + [VMEM] * 3 + [HBM] * 6 + [ANY] * pieces,
         out_specs=[HBM] * pieces + [VMEM] * len(more),
         scratch_shapes=[
             pltpu.VMEM((taps, LANES, LANES), jnp.bfloat16),
@@ -306,30 +301,34 @@
     )(scalars, selection, *held, *features, *halos, *counts, *w_parts)
 
 
-def sum_kernel(scale, scalars, *rest):
+def sum_kernel(scale, blocks, scalars, *rest):
     parts, (mine_ref, other_ref, rows) = rest[:-3], rest[-3:]
     core = scalars[0]
     share = mine_ref.shape[0]
-    for b in range(parts[0].shape[0]):
-        total = parts[0][b].astype(jnp.float32)
-        for part in parts[1:]:
-            total += part[b].astype(jnp.float32)
-        rows[b * LANES : (b + 1) * LANES, :] = total.T * scale
+    pieces = len(parts) // blocks
+    for j in range(blocks):
+        for b in range(parts[0].shape[0]):
+            total = parts[j * pieces][b].astype(jnp.float32)
+            for part in parts[j * pieces + 1 : (j + 1) * pieces]:
+                total += part[b].astype(jnp.float32)
+            rows[b * LANES : (b + 1) * LANES, j * LANES : (j + 1) * LANES] = total.T * scale
     mine_ref[...] = rows[pl.ds(pl.multiple_of(core * share, 8), share), :]
     other_ref[...] = rows[pl.ds(pl.multiple_of((1 - core) * share, 8), share), :]
 
 
-def summed(scalars, parts, share, scale):
-    shape = jax.ShapeDtypeStruct((share, LANES), jnp.float32)
-    return pl.pallas_call(
-        functools.partial(sum_kernel, scale),
+def summed(scalars, arrived, share, scale):
+    blocks = len(arrived)
+    parts = [part for pieces in arrived for part in pieces]
+    shape = jax.ShapeDtypeStruct((share, blocks * LANES), jnp.float32)
+    return pl.pallas_call(
+        functools.partial(sum_kernel, scale, blocks),
         in_specs=[SMEM] + [VMEM] * len(parts),
         out_specs=[VMEM] * 2,
         out_shape=[shape, shape],
-        scratch_shapes=[pltpu.VMEM((2 * share, LANES), jnp.float32)],
+        scratch_shapes=[pltpu.VMEM((2 * share, blocks * LANES), jnp.float32)],
         compiler_params=ALL_VMEM,
         name="summed",
-        cost_estimate=pl.CostEstimate(flops=0, bytes_accessed=8 * share * LANES, transcendentals=0),
+        cost_estimate=pl.CostEstimate(flops=0, bytes_accessed=8 * share * blocks * LANES, transcendentals=0),
     )(scalars, *parts)
 
 
@@ -340,7 +339,7 @@
     copies = []
     for i, part in enumerate(parts):
         side = core if i % 2 == 0 else 1 - core
-        lanes = pl.ds(pl.multiple_of(side * core_genes + (base + i // 2) * LANES, LANES), LANES)
+        lanes = pl.ds(pl.multiple_of(side * core_genes + base * LANES, LANES), part.shape[1])
         copies.append(pltpu.make_async_copy(part, out.at[:, lanes], sem.at[i]))
     for copy in copies:
         copy.start()
@@ -374,25 +373,21 @@
     gene_total = local_genes * gene_parts
     norm_scale = 1.0 / math.sqrt(row_count * tiles * col_count)
     bins = row_count * col_count
-    me, gene_part = lax.axis_index("tile"), lax.axis_index("gene")
-    core, chip, parity = me & 1, me >> 1, gene_part & 1
-    scalars = jnp.stack([core, chip, parity]).astype(jnp.int32)
+    me = lax.axis_index("tile")
+    core, chip = me & 1, me >> 1
+    scalars = jnp.stack([core, chip]).astype(jnp.int32)
     core_genes = local_genes // 2
     core_blocks = core_genes // LANES
     share = weights.shape[0]
     chips = tiles // 2
-    planned = chips == 4 and (2 * share) % LANES == 0 and len(ROUTES) == core_blocks
+    planned = chips == 4 and (2 * share) % LANES == 0 and sum(map(len, GROUPS)) == core_blocks
 
     flat = features.reshape(bins, width)
     if planned:
         came = swap_cores(weights, tiles)
-    edge = lax.dynamic_slice(
-        features, (core * (row_count - 1), 0, parity * (width // 2)), (1, col_count, width // 2)
-    ).reshape(col_count, width // 2)
+    edge = lax.dynamic_slice_in_dim(flat, core * (bins - col_count), col_count, 0)
     outward = [(t, t + 1) for t in range(1, tiles - 1, 2)] + [(t, t - 1) for t in range(2, tiles, 2)]
-    beside = [(g, g ^ 1) for g in range(gene_parts)]
     halo = lax.ppermute(edge, "tile", outward)
-    halo_z = lax.ppermute(halo, "gene", beside)
     other_rows = swap_cores(flat, tiles)
     own_counts, away_counts, own_library = small_counts(scalars, counts)
     other_library = swap_cores(own_library, tiles)
@@ -400,36 +395,37 @@
 
     gathered = []
     if planned:
-        for b, part in enumerate(turn_weights(scalars, weights, came)):
-            got = {p: exchanged(part, p, tiles) for p in (1, 2)}
-            source, way = {"direct": (part, 3), "x": (got[1], 2), "y": (got[2], 1)}[ROUTES[b]]
-            gathered.append([part, got[1], got[2], exchanged(source, way, tiles)])
+        for part in turn_weights(scalars, weights, came):
+            got = {p: exchanged(part, p, tiles) for p in (3, 1, 2)}
+            parts = [part] + [got[p] for p in (1, 2, 3)]
+            gathered += [(parts, j) for j in range(part.shape[0])]
     else:
         full = lax.all_gather(weights, "tile", axis=0, tiled=True)
         mine = lax.dynamic_slice_in_dim(full, core * core_genes, core_genes, 1)
-        gathered = [[part] for part in mine.reshape(-1, LANES, core_blocks, LANES).transpose(2, 0, 3, 1)]
+        full = mine.reshape(-1, LANES, core_blocks, LANES).transpose(2, 0, 3, 1)
+        gathered = [([full], j) for j in range(core_blocks)]
 
     library = jnp.concatenate([own_library, other_library], axis=0)
-    if gene_parts <= 4:
-        around = [
-            lax.ppermute(library, "gene", [(g, (g + i) % gene_parts) for g in range(gene_parts)])
-            for i in range(1, gene_parts)
-        ]
-        libraries = jnp.stack([library] + around)
+    bits = gene_parts.bit_length() - 1
+    if gene_parts == 1 << bits and bits > 0:
+        for bit in range(bits):
+            came = lax.ppermute(library, "gene", [(g, g ^ (1 << bit)) for g in range(gene_parts)])
+            libraries = (library, came)
+            library = library + came if bit + 1 < bits else library
     else:
-        libraries = lax.psum(library, "gene")[None]
-    halos = (halo, halo_z, swap_cores(halo, tiles), swap_cores(halo_z, tiles))
+        libraries = (lax.psum(library, "gene"), jnp.zeros_like(library))
+    halos = (halo, swap_cores(halo, tiles))
 
     sources = tuple(
-        tuple(pltpu.with_memory_space_constraint(x, pltpu.HBM) for x in group)
+        tuple(in_hbm(x) for x in group)
         for group in ((flat, other_rows), halos, (own_counts, other_counts))
     )
     *held, factors = load_block(scalars, selection, *sources, libraries, 0, row_count, col_count, gene_total)
     gradients = []
-    for b, w_parts in enumerate(gathered):
+    for b, (w_parts, offset) in enumerate(gathered):
         following = b + 1 if b + 1 < core_blocks else None
         results = block_gradient(
-            scalars, selection, (*held, factors), *sources, w_parts, following, row_count, col_count
+            scalars, selection, (*held, factors), *sources, w_parts, offset, following, row_count, col_count
         )
         gradients.append(results[: len(w_parts)])
         held = results[len(w_parts) :]
@@ -444,12 +440,12 @@
     arrived = []
     for own, *others in gradients:
         arrived.append([own] + [exchanged(others[p - 1], p, tiles) for p in (1, 2, 3)])
-    parts = []
-    for pieces in arrived:
-        mine, other = summed(scalars, pieces, share, norm_scale)
-        parts += [mine, swap_cores(other, tiles)]
-    out = placed(scalars, parts[:-2], 0, None, share, local_genes)
-    return placed(scalars, parts[-2:], core_blocks - 1, out, share, local_genes)
+    out = None
+    for group in (range(core_blocks - 1), range(core_blocks - 1, core_blocks)):
+        mine, other = summed(scalars, [arrived[b] for b in group], share, norm_scale)
+        parts = (mine, swap_cores(other, tiles))
+        out = placed(scalars, parts, group[0], out, share, local_genes)
+    return out
 
 
 def solution(mesh):

time: 165 us -> 193 us (1.17)
  waiting for transfers between devices: 19.6 us -> 38.2 us
  local copies, waits for them, and re-layouts: 3.49 us -> 12.7 us
    ppermute x24 -> x21, waiting for transfers between devices: 14.3 us -> 34.1 us  [exchanged(): return lax.ppermute(x, 'tile', [(t, t ^ 2 * piece) for t in range(count)])]
    unnamed x43 -> x47, local copies, waits for them, and re-layouts: 2.47 us -> 11.6 us
    ppermute x10 -> x7, starting transfers between devices: 15 us -> 21.2 us  [swap_cores(): return lax.ppermute(x, 'tile', [(t, t ^ 1) for t in range(count)])]
    ppermute x4 -> x2, starting transfers between devices: 9.48 us -> 4.82 us  [per_device(): lax.ppermute(library, 'gene', [(g, g ^ 1 << bit) for g in range(gene_part...]
    pallas_call x4 -> x2, Pallas kernels: 9.33 us -> 6.09 us  [summed(): pl.pallas_call(functools.partial(sum_kernel, scale, blocks), in_specs=[SM...]
    ppermute x4 -> x2, waiting for transfers between devices: 4.21 us -> 1.9 us  [per_device(): lax.ppermute(library, 'gene', [(g, g ^ 1 << bit) for g in range(gene_part...]
    ppermute x24 -> x21, starting transfers between devices: 31.1 us -> 30.1 us  [exchanged(): return lax.ppermute(x, 'tile', [(t, t ^ 2 * piece) for t in range(count)])]
  transfers between devices with their start and end apart: 39 -> 31, of which waited for: 6 -> 10; matrix products, arithmetic and copies ran while one was open for 2% -> 2% of each run, Pallas kernels for 49% -> 39%
where the time goes in v2:
time: 193 us
  Pallas kernels  81.4 us (42%)
  starting transfers between devices  57.8 us (30%)
  waiting for transfers between devices  38.2 us (20%)
  local copies, waits for them, and re-layouts  12.7 us (7%)
  other arithmetic  2.05 us (1%)
    pallas_call x4, Pallas kernels, block_gradient(): pl.pallas_call(functools.partial(grad_kernel, plan), in_specs=[SMEM] * 2...  55.2 us
    ppermute x21, waiting for transfers between devices, exchanged(): return lax.ppermute(x, 'tile', [(t, t ^ 2 * piece) for t in range(count)])  34.1 us
    ppermute x21, starting transfers between devices, exchanged(): return lax.ppermute(x, 'tile', [(t, t ^ 2 * piece) for t in range(count)])  30.1 us
    ppermute x7, starting transfers between devices, swap_cores(): return lax.ppermute(x, 'tile', [(t, t ^ 1) for t in range(count)])  21.2 us
    unnamed x47, local copies, waits for them, and re-layouts  11.6 us
    pallas_call x1, Pallas kernels, small_counts(): pl.pallas_call(counts_kernel, grid_spec=pltpu.PrefetchScalarGridSpec(num_...  8.49 us
    pallas_call x2, Pallas kernels, summed(): pl.pallas_call(functools.partial(sum_kernel, scale, blocks), in_specs=[SM...  6.09 us
    ppermute x2, starting transfers between devices, per_device(): lax.ppermute(library, 'gene', [(g, g ^ 1 << bit) for g in range(gene_part...  4.82 us
  transfers between devices with their start and end apart: 31, of which 10 were waited for; matrix products, arithmetic and copies ran while one was open for 2% of the time, Pallas kernels for 39%

profile of v2, /device:TPU:0, one launch (start us, length us, event | category | flops | bytes accessed | tf_op | source)
XLA Modules:
  0.0 192.6 jit_solution(646920474150829026)
XLA Ops:
  1.1 8.5 %small_counts.1 = (bf16[2048,512]{1,0:T(8,128)(2,1)}, bf16[2048,512]{1,0:T(8,128)(2,1)}, f32[1,2048]{1,0:T(1,128)}) custom-call(s32[2]{0:T(128)} %pad_add_fusion.scalars, s32[8,256,1024]{2,1,0:T(8,128)} %counts_ref.1), custom_call_target="tpu_custom_call" | custom-call | bytes 12582912 | tf_op jit(solution)/shard_map/small_counts/pallas_call | solution.py:60
  12.4 3.5 %collective-permute-start.7 = (bf16[576,1024]{1,0:T(8,128)(2,1)}, bf16[576,1024]{1,0:T(8,128)(2,1)}, u32[]{:S(2)}, u32[]{:S(2)}) collective-permute-start(bf16[576,1024]{1,0:T(8,128)(2,1)} %mine_ref.1), channel_id=1, source_target_pairs={{0,4},{4,0},{8,12},{12,8},{16,20},{20,16},{24,28},{28,24},{1,5},{5... | collective-permute-start | bytes 3538952 | tf_op jit(solution)/shard_map/ppermute | solution.py:30
  15.9 17.2 %collective-permute-start.2 = (bf16[256,1536]{1,0:T(8,128)(2,1)}, bf16[256,1536]{1,0:T(8,128)(2,1)}, u32[]{:S(2)}, u32[]{:S(2)}) collective-permute-start(bf16[256,1536]{1,0:T(8,128)(2,1)} %collective-permute-done.1.rest_2_), channel_id=1, source_target_pairs={{0,4},{4,0},{8,12},{12,8},{16,20},{20,16},{24,28},{28,24},{1,5},{5... | collective-permute-start | bytes 2359304 | tf_op jit(solution)/shard_map/ppermute | solution.py:30
  40.6 2.9 %collective-permute-start.6 = (f32[2,2048]{1,0:T(2,128)S(1)}, f32[2,2048]{1,0:T(2,128)S(1)}, u32[]{:S(2)}, u32[]{:S(2)}) collective-permute-start(f32[2,2048]{1,0:T(2,128)S(1)} %fusion.rest_6_), channel_id=1, source_target_pairs={{0,2},{1,3},{2,0},{3,1},{4,6},{5,7},{6,4},{7,5},{8,10},{9,11},{10,... | collective-permute-start | bytes 49160 | tf_op jit(solution)/shard_map/ppermute | solution.py:412
  43.5 3.5 %turn_weights.1 = (bf16[1,9,128,128]{3,2,1,0:T(8,128)(2,1)}, bf16[1,9,128,128]{3,2,1,0:T(8,128)(2,1)}, bf16[2,9,128,128]{3,2,1,0:T(8,128)(2,1)}) custom-call(s32[2]{0:T(128)} %pad_add_fusion.scalars, bf16[576,1024]{1,0:T(8,128)(2,1)} %mine_ref.1, bf16[576,1024]{1,0:T(8,128)(2,1)} %collective-permute-done.7.came_ref), custom_call_target="tpu_custom_call" | custom-call | bytes 3538944 | tf_op jit(solution)/shard_map/turn_weights/pallas_call | solution.py:93
  47.0 3.5 %collective-permute-start.10 = (bf16[1,9,128,128]{3,2,1,0:T(8,128)(2,1)}, bf16[1,9,128,128]{3,2,1,0:T(8,128)(2,1)S(1)}, u32[]{:S(2)}, u32[]{:S(2)}) collective-permute-start(bf16[1,9,128,128]{3,2,1,0:T(8,128)(2,1)} %get-tuple-element.46.rest_6_), channel_id=1, source_target_pairs={{0,24},{4,28},{8,16},{12,20},{16,8},{20,12},{24,0},{28,4},{1,25},{... | collective-permute-start | bytes 884744 | tf_op jit(solution)/shard_map/ppermute | solution.py:366
  51.6 2.4 %collective-permute-start.16 = (bf16[1,9,128,128]{3,2,1,0:T(8,128)(2,1)}, bf16[1,9,128,128]{3,2,1,0:T(8,128)(2,1)S(1)}, u32[]{:S(2)}, u32[]{:S(2)}) collective-permute-start(bf16[1,9,128,128]{3,2,1,0:T(8,128)(2,1)} %get-tuple-element.53.rest_6_), channel_id=1, source_target_pairs={{0,24},{4,28},{8,16},{12,20},{16,8},{20,12},{24,0},{28,4},{1,25},{... | collective-permute-start | bytes 884744 | tf_op jit(solution)/shard_map/ppermute | solution.py:366
  55.1 3.6 %load_block.1 = (bf16[4608,512]{1,0:T(8,128)(2,1)S(1)}, bf16[4096,128]{1,0:T(8,128)(2,1)S(1)}, f32[1,4096]{1,0:T(1,128)S(1)}) custom-call(s32[2]{0:T(128)S(1)} %copy-done, s32[8,4]{1,0:T(8,128)S(1)} %copy.7.selection, bf16[2048,1536]{1,0:T(8,128)(2,1)} %bitcast.5, bf16[2048,1536]{1,0:T(8,128)(2,1)} %collective-permute-done.rest_1_, ...), custom_call_target="tpu_custom_call" | custom-call | bytes 12582912 | tf_op jit(solution)/shard_map/load_block/pallas_call | solution.py:171
  58.7 2.3 %collective-permute-start.14 = (bf16[1,9,128,128]{3,2,1,0:T(8,128)(2,1)S(1)}, bf16[1,9,128,128]{3,2,1,0:T(8,128)(2,1)S(1)}, u32[]{:S(2)}, u32[]{:S(2)}) collective-permute-start(bf16[1,9,128,128]{3,2,1,0:T(8,128)(2,1)S(1)} %copy-done.9), channel_id=1, source_target_pairs={{0,8},{4,12},{8,0},{12,4},{16,24},{20,28},{24,16},{28,20},{1,9},{5... | collective-permute-start | bytes 884744 | tf_op jit(solution)/shard_map/ppermute | solution.py:366
  61.0 3.9 %collective-permute-done.9.rest_8_ = bf16[1,9,128,128]{3,2,1,0:T(8,128)(2,1)S(1)} collective-permute-done((bf16[1,9,128,128]{3,2,1,0:T(8,128)(2,1)}, bf16[1,9,128,128]{3,2,1,0:T(8,128)(2,1)S(1)}, u32[]{:S(2)}, u32[]{:S(2)}) %collective-permute-start.9) | collective-permute-done | bytes 294944 | tf_op jit(solution)/shard_map/ppermute | solution.py:366
  65.0 2.9 %collective-permute-start.22 = (bf16[2,9,128,128]{3,2,1,0:T(8,128)(2,1)S(1)}, bf16[2,9,128,128]{3,2,1,0:T(8,128)(2,1)S(1)}, u32[]{:S(2)}, u32[]{:S(2)}) collective-permute-start(bf16[2,9,128,128]{3,2,1,0:T(8,128)(2,1)S(1)} %copy-done.2), channel_id=1, source_target_pairs={{0,24},{4,28},{8,16},{12,20},{16,8},{20,12},{24,0},{28,4},{1,25},{... | collective-permute-start | bytes 1769480 | tf_op jit(solution)/shard_map/ppermute | solution.py:366
  68.9 13.8 %block_gradient.4 = (bf16[9,128,128]{2,1,0:T(8,128)(2,1)}, bf16[9,128,128]{2,1,0:T(8,128)(2,1)}, bf16[9,128,128]{2,1,0:T(8,128)(2,1)}, bf16[9,128,128]{2,1,0:T(8...) custom-call(s32[2]{0:T(128)S(1)} %copy-done, s32[8,4]{1,0:T(8,128)S(1)} %copy.7.selection, ...), custom_call_target="tpu_custom_call" | custom-call | flops 9663676416 | bytes 10485760 | tf_op jit(solution)/shard_map/block_gradient/pallas_call | solution.py:280
  85.8 13.8 %block_gradient.5 = (bf16[9,128,128]{2,1,0:T(8,128)(2,1)}, bf16[9,128,128]{2,1,0:T(8,128)(2,1)}, bf16[9,128,128]{2,1,0:T(8,128)(2,1)}, bf16[9,128,128]{2,1,0:T(8...) custom-call(s32[2]{0:T(128)S(1)} %copy-done, s32[8,4]{1,0:T(8,128)S(1)} %copy.7.selection, ...), custom_call_target="tpu_custom_call" | custom-call | flops 9663676416 | bytes 10485760 | tf_op jit(solution)/shard_map/block_gradient/pallas_call | solution.py:280
  100.9 2.5 %collective-permute-start.17 = (bf16[9,128,128]{2,1,0:T(8,128)(2,1)}, bf16[9,128,128]{2,1,0:T(8,128)(2,1)}, u32[]{:S(2)}, u32[]{:S(2)}) collective-permute-start(bf16[9,128,128]{2,1,0:T(8,128)(2,1)} %get-tuple-element.55), channel_id=1, source_target_pairs={{0,8},{4,12},{8,0},{12,4},{16,24},{20,28},{24,16},{28,20},{1,9},{5... | collective-permute-start | bytes 884744 | tf_op jit(solution)/shard_map/ppermute | solution.py:366
  104.1 13.6 %block_gradient.6 = (bf16[9,128,128]{2,1,0:T(8,128)(2,1)}, bf16[9,128,128]{2,1,0:T(8,128)(2,1)}, bf16[9,128,128]{2,1,0:T(8,128)(2,1)}, bf16[9,128,128]{2,1,0:T(8...) custom-call(s32[2]{0:T(128)S(1)} %copy-done, s32[8,4]{1,0:T(8,128)S(1)} %copy.7.selection, ...), custom_call_target="tpu_custom_call" | custom-call | flops 9663676416 | bytes 10485760 | tf_op jit(solution)/shard_map/block_gradient/pallas_call | solution.py:280
  126.8 5.2 %collective-permute-done.19.rest_7_ = bf16[9,128,128]{2,1,0:T(8,128)(2,1)} collective-permute-done((bf16[9,128,128]{2,1,0:T(8,128)(2,1)S(1)}, bf16[9,128,128]{2,1,0:T(8,128)(2,1)}, u32[]{:S(2)}, u32[]{:S(2)}) %collective-permute-start.19) | collective-permute-done | bytes 294944 | tf_op jit(solution)/shard_map/ppermute | solution.py:366
  131.9 6.4 %collective-permute-done.23.rest_9_ = bf16[9,128,128]{2,1,0:T(8,128)(2,1)} collective-permute-done((bf16[9,128,128]{2,1,0:T(8,128)(2,1)}, bf16[9,128,128]{2,1,0:T(8,128)(2,1)}, u32[]{:S(2)}, u32[]{:S(2)}) %collective-permute-start.23) | collective-permute-done | bytes 294944 | tf_op jit(solution)/shard_map/ppermute | solution.py:366
  138.4 3.8 %collective-permute-done.25.rest_11_ = bf16[9,128,128]{2,1,0:T(8,128)(2,1)} collective-permute-done((bf16[9,128,128]{2,1,0:T(8,128)(2,1)}, bf16[9,128,128]{2,1,0:T(8,128)(2,1)}, u32[]{:S(2)}, u32[]{:S(2)}) %collective-permute-start.25) | collective-permute-done | bytes 294944 | tf_op jit(solution)/shard_map/ppermute | solution.py:366
  142.2 3.8 %summed.2 = (f32[576,384]{1,0:T(8,128)}, f32[576,384]{1,0:T(8,128)}) custom-call(s32[2]{0:T(128)} %pad_add_fusion.scalars, bf16[9,128,128]{2,1,0:T(8,128)(2,1)} %get-tuple-element.47.rest_0_, bf16[9,128,128]{2,1,0:T(8,128)(2,1)} %copy-done.16, bf16[9,128,128]{2,1,0:T(8,128)(2,1)} %collective-permute-done.12.rest_2_, ...), custom_call_target="tpu_custom_call" | custom-call | bytes 1769472 | tf_op jit(solution)/shard_map/summed/pallas_call | solution.py:323
  149.1 2.3 %copy-done.12 = bf16[4608,512]{1,0:T(8,128)(2,1)S(1)} copy-done((bf16[4608,512]{1,0:T(8,128)(2,1)S(1)}, bf16[4608,512]{1,0:T(8,128)(2,1)}, u32[]{:S(2)}) %copy-start.12) | copy-done | bytes 4718616
  152.7 13.9 %block_gradient.7 = (bf16[9,128,128]{2,1,0:T(8,128)(2,1)}, bf16[9,128,128]{2,1,0:T(8,128)(2,1)}, bf16[9,128,128]{2,1,0:T(8,128)(2,1)}, bf16[9,128,128]{2,1,0:T(8,128)(2,1)}) custom-call(s32[2]{0:T(128)S(1)} %copy-done.1, s32[8,4]{1,0:T(8,128)S(1)} %copy.7.selection, bf16[4608,512]{1,0:T(8,128)(2,1)S(1)} %copy-done.12, bf16[4096,128]{1,0:T(8,128)(2,1)S(1)} %copy-done.14, ...), custom_call_target="tpu_custom_call" | custom-call | flops 9663676416 | bytes 10485760 | tf_op jit(solution)/shard_map/block_gradient/pallas_call | solution.py:280
  170.2 6.6 %collective-permute-done.27.rest_1_ = bf16[9,128,128]{2,1,0:T(8,128)(2,1)S(1)} collective-permute-done((bf16[9,128,128]{2,1,0:T(8,128)(2,1)}, bf16[9,128,128]{2,1,0:T(8,128)(2,1)S(1)}, u32[]{:S(2)}, u32[]{:S(2)}) %collective-permute-start.27) | collective-permute-done | bytes 294944 | tf_op jit(solution)/shard_map/ppermute | solution.py:366
  176.8 7.2 %collective-permute-done.28.rest_2_ = bf16[9,128,128]{2,1,0:T(8,128)(2,1)S(1)} collective-permute-done((bf16[9,128,128]{2,1,0:T(8,128)(2,1)}, bf16[9,128,128]{2,1,0:T(8,128)(2,1)S(1)}, u32[]{:S(2)}, u32[]{:S(2)}) %collective-permute-start.28) | collective-permute-done | bytes 294944 | tf_op jit(solution)/shard_map/ppermute | solution.py:366
  187.1 2.7 %placed.2.rest_0_ = f32[576,1024]{1,0:T(8,128)} custom-call(s32[2]{0:T(128)} %pad_add_fusion.scalars, f32[576,384]{1,0:T(8,128)} %get-tuple-element.65.rest_0_, f32[576,384]{1,0:T(8,128)} %collective-permute-done.26.rest_1_), custom_call_target="tpu_custom_call" | custom-call | bytes 1179648 | tf_op jit(solution)/shard_map/placed/pallas_call | solution.py:352
  (100 shorter events, 42.4 us)
Async XLA Ops:
  0.0 54.0 %collective-permute-start = (bf16[2048,1536]{1,0:T(8,128)(2,1)}, bf16[2048,1536]{1,0:T(8,128)(2,1)}, u32[]{:S(2)}, u32[]{:S(2)}) collective-permute-start(bf16[2048,1536]{1,0:T(8,128)(2,1)} %bitcast.3), channel_id=1, source_target_pairs={{0,4},{4,0},{8,12},{12,8},{16,20},{20,16},{24,28},{28,24},{1,5},{5... | collective-permute-start | bytes 18874376 | tf_op jit(solution)/shard_map/ppermute | solution.py:30
  9.6 42.0 %collective-permute-start.3 = (bf16[2048,512]{1,0:T(8,128)(2,1)}, bf16[2048,512]{1,0:T(8,128)(2,1)}, u32[]{:S(2)}, u32[]{:S(2)}) collective-permute-start(bf16[2048,512]{1,0:T(8,128)(2,1)} %get-tuple-element.41), channel_id=1, source_target_pairs={{0,4},{4,0},{8,12},{12,8},{16,20},{20,16},{24,28},{28,24},{1,5},{5... | collective-permute-start | bytes 6291464 | tf_op jit(solution)/shard_map/ppermute | solution.py:30
  12.4 31.1 %collective-permute-start.7 = (bf16[576,1024]{1,0:T(8,128)(2,1)}, bf16[576,1024]{1,0:T(8,128)(2,1)}, u32[]{:S(2)}, u32[]{:S(2)}) collective-permute-start(bf16[576,1024]{1,0:T(8,128)(2,1)} %mine_ref.1), channel_id=1, source_target_pairs={{0,4},{4,0},{8,12},{12,8},{16,20},{20,16},{24,28},{28,24},{1,5},{5... | collective-permute-start | bytes 3538952 | tf_op jit(solution)/shard_map/ppermute | solution.py:30
  15.9 35.6 %collective-permute-start.2 = (bf16[256,1536]{1,0:T(8,128)(2,1)}, bf16[256,1536]{1,0:T(8,128)(2,1)}, u32[]{:S(2)}, u32[]{:S(2)}) collective-permute-start(bf16[256,1536]{1,0:T(8,128)(2,1)} %collective-permute-done.1.rest_2_), channel_id=1, source_target_pairs={{0,4},{4,0},{8,12},{12,8},{16,20},{20,16},{24,28},{28,24},{1,5},{5... | collective-permute-start | bytes 2359304 | tf_op jit(solution)/shard_map/ppermute | solution.py:30
  47.0 11.7 %collective-permute-start.10 = (bf16[1,9,128,128]{3,2,1,0:T(8,128)(2,1)}, bf16[1,9,128,128]{3,2,1,0:T(8,128)(2,1)S(1)}, u32[]{:S(2)}, u32[]{:S(2)}) collective-permute-start(bf16[1,9,128,128]{3,2,1,0:T(8,128)(2,1)} %get-tuple-element.46.rest_6_), channel_id=1, source_target_pairs={{0,24},{4,28},{8,16},{12,20},{16,8},{20,12},{24,0},{28,4},{1,25},{... | collective-permute-start | bytes 884744 | tf_op jit(solution)/shard_map/ppermute | solution.py:366
  50.5 14.5 %collective-permute-start.9 = (bf16[1,9,128,128]{3,2,1,0:T(8,128)(2,1)}, bf16[1,9,128,128]{3,2,1,0:T(8,128)(2,1)S(1)}, u32[]{:S(2)}, u32[]{:S(2)}) collective-permute-start(bf16[1,9,128,128]{3,2,1,0:T(8,128)(2,1)} %get-tuple-element.46.rest_6_), channel_id=1, source_target_pairs={{0,16},{4,20},{8,24},{12,28},{16,0},{20,4},{24,8},{28,12},{1,17},{... | collective-permute-start | bytes 884744 | tf_op jit(solution)/shard_map/ppermute | solution.py:366
  51.5 16.3 %collective-permute-start.8 = (bf16[1,9,128,128]{3,2,1,0:T(8,128)(2,1)}, bf16[1,9,128,128]{3,2,1,0:T(8,128)(2,1)S(1)}, u32[]{:S(2)}, u32[]{:S(2)}) collective-permute-start(bf16[1,9,128,128]{3,2,1,0:T(8,128)(2,1)} %get-tuple-element.46.rest_6_), channel_id=1, source_target_pairs={{0,8},{4,12},{8,0},{12,4},{16,24},{20,28},{24,16},{28,20},{1,9},{5... | collective-permute-start | bytes 884744 | tf_op jit(solution)/shard_map/ppermute | solution.py:366
  51.6 31.1 %collective-permute-start.16 = (bf16[1,9,128,128]{3,2,1,0:T(8,128)(2,1)}, bf16[1,9,128,128]{3,2,1,0:T(8,128)(2,1)S(1)}, u32[]{:S(2)}, u32[]{:S(2)}) collective-permute-start(bf16[1,9,128,128]{3,2,1,0:T(8,128)(2,1)} %get-tuple-element.53.rest_6_), channel_id=1, source_target_pairs={{0,24},{4,28},{8,16},{12,20},{16,8},{20,12},{24,0},{28,4},{1,25},{... | collective-permute-start | bytes 884744 | tf_op jit(solution)/shard_map/ppermute | solution.py:366
  54.0 28.7 %collective-permute-start.15 = (bf16[1,9,128,128]{3,2,1,0:T(8,128)(2,1)}, bf16[1,9,128,128]{3,2,1,0:T(8,128)(2,1)S(1)}, u32[]{:S(2)}, u32[]{:S(2)}) collective-permute-start(bf16[1,9,128,128]{3,2,1,0:T(8,128)(2,1)} %get-tuple-element.53.rest_6_), channel_id=1, source_target_pairs={{0,16},{4,20},{8,24},{12,28},{16,0},{20,4},{24,8},{28,12},{1,17},{... | collective-permute-start | bytes 884744 | tf_op jit(solution)/shard_map/ppermute | solution.py:366
  58.7 26.1 %collective-permute-start.14 = (bf16[1,9,128,128]{3,2,1,0:T(8,128)(2,1)S(1)}, bf16[1,9,128,128]{3,2,1,0:T(8,128)(2,1)S(1)}, u32[]{:S(2)}, u32[]{:S(2)}) collective-permute-start(bf16[1,9,128,128]{3,2,1,0:T(8,128)(2,1)S(1)} %copy-done.9), channel_id=1, source_target_pairs={{0,8},{4,12},{8,0},{12,4},{16,24},{20,28},{24,16},{28,20},{1,9},{5... | collective-permute-start | bytes 884744 | tf_op jit(solution)/shard_map/ppermute | solution.py:366
  65.0 34.7 %collective-permute-start.22 = (bf16[2,9,128,128]{3,2,1,0:T(8,128)(2,1)S(1)}, bf16[2,9,128,128]{3,2,1,0:T(8,128)(2,1)S(1)}, u32[]{:S(2)}, u32[]{:S(2)}) collective-permute-start(bf16[2,9,128,128]{3,2,1,0:T(8,128)(2,1)S(1)} %copy-done.2), channel_id=1, source_target_pairs={{0,24},{4,28},{8,16},{12,20},{16,8},{20,12},{24,0},{28,4},{1,25},{... | collective-permute-start | bytes 1769480 | tf_op jit(solution)/shard_map/ppermute | solution.py:366
  67.8 33.0 %collective-permute-start.21 = (bf16[2,9,128,128]{3,2,1,0:T(8,128)(2,1)S(1)}, bf16[2,9,128,128]{3,2,1,0:T(8,128)(2,1)S(1)}, u32[]{:S(2)}, u32[]{:S(2)}) collective-permute-start(bf16[2,9,128,128]{3,2,1,0:T(8,128)(2,1)S(1)} %copy-done.2), channel_id=1, source_target_pairs={{0,16},{4,20},{8,24},{12,28},{16,0},{20,4},{24,8},{28,12},{1,17},{... | collective-permute-start | bytes 1769480 | tf_op jit(solution)/shard_map/ppermute | solution.py:366
  82.7 21.0 %collective-permute-start.20 = (bf16[2,9,128,128]{3,2,1,0:T(8,128)(2,1)S(1)}, bf16[2,9,128,128]{3,2,1,0:T(8,128)(2,1)S(1)}, u32[]{:S(2)}, u32[]{:S(2)}) collective-permute-start(bf16[2,9,128,128]{3,2,1,0:T(8,128)(2,1)S(1)} %copy-done.2), channel_id=1, source_target_pairs={{0,8},{4,12},{8,0},{12,4},{16,24},{20,28},{24,16},{28,20},{1,9},{5... | collective-permute-start | bytes 1769480 | tf_op jit(solution)/shard_map/ppermute | solution.py:366
  82.8 38.2 %collective-permute-start.11 = (bf16[9,128,128]{2,1,0:T(8,128)(2,1)}, bf16[9,128,128]{2,1,0:T(8,128)(2,1)S(1)}, u32[]{:S(2)}, u32[]{:S(2)}) collective-permute-start(bf16[9,128,128]{2,1,0:T(8,128)(2,1)} %get-tuple-element.48), channel_id=1, source_target_pairs={{0,8},{4,12},{8,0},{12,4},{16,24},{20,28},{24,16},{28,20},{1,9},{5... | collective-permute-start | bytes 884744 | tf_op jit(solution)/shard_map/ppermute | solution.py:366
  84.8 38.5 %collective-permute-start.12 = (bf16[9,128,128]{2,1,0:T(8,128)(2,1)}, bf16[9,128,128]{2,1,0:T(8,128)(2,1)}, u32[]{:S(2)}, u32[]{:S(2)}) collective-permute-start(bf16[9,128,128]{2,1,0:T(8,128)(2,1)} %get-tuple-element.49), channel_id=1, source_target_pairs={{0,16},{4,20},{8,24},{12,28},{16,0},{20,4},{24,8},{28,12},{1,17},{... | collective-permute-start | bytes 884744 | tf_op jit(solution)/shard_map/ppermute | solution.py:366
  99.7 24.4 %collective-permute-start.13 = (bf16[9,128,128]{2,1,0:T(8,128)(2,1)S(1)}, bf16[9,128,128]{2,1,0:T(8,128)(2,1)}, u32[]{:S(2)}, u32[]{:S(2)}) collective-permute-start(bf16[9,128,128]{2,1,0:T(8,128)(2,1)S(1)} %copy-done.21), channel_id=1, source_target_pairs={{0,24},{4,28},{8,16},{12,20},{16,8},{20,12},{24,0},{28,4},{1,25},{... | collective-permute-start | bytes 884744 | tf_op jit(solution)/shard_map/ppermute | solution.py:366
  100.9 23.6 %collective-permute-start.17 = (bf16[9,128,128]{2,1,0:T(8,128)(2,1)}, bf16[9,128,128]{2,1,0:T(8,128)(2,1)}, u32[]{:S(2)}, u32[]{:S(2)}) collective-permute-start(bf16[9,128,128]{2,1,0:T(8,128)(2,1)} %get-tuple-element.55), channel_id=1, source_target_pairs={{0,8},{4,12},{8,0},{12,4},{16,24},{20,28},{24,16},{28,20},{1,9},{5... | collective-permute-start | bytes 884744 | tf_op jit(solution)/shard_map/ppermute | solution.py:366
  103.7 23.1 %collective-permute-start.18 = (bf16[9,128,128]{2,1,0:T(8,128)(2,1)}, bf16[9,128,128]{2,1,0:T(8,128)(2,1)}, u32[]{:S(2)}, u32[]{:S(2)}) collective-permute-start(bf16[9,128,128]{2,1,0:T(8,128)(2,1)} %get-tuple-element.56), channel_id=1, source_target_pairs={{0,16},{4,20},{8,24},{12,28},{16,0},{20,4},{24,8},{28,12},{1,17},{... | collective-permute-start | bytes 884744 | tf_op jit(solution)/shard_map/ppermute | solution.py:366
  123.3 15.1 %collective-permute-start.23 = (bf16[9,128,128]{2,1,0:T(8,128)(2,1)}, bf16[9,128,128]{2,1,0:T(8,128)(2,1)}, u32[]{:S(2)}, u32[]{:S(2)}) collective-permute-start(bf16[9,128,128]{2,1,0:T(8,128)(2,1)} %get-tuple-element.62), channel_id=1, source_target_pairs={{0,8},{4,12},{8,0},{12,4},{16,24},{20,28},{24,16},{28,20},{1,9},{5... | collective-permute-start | bytes 884744 | tf_op jit(solution)/shard_map/ppermute | solution.py:366
  124.1 14.3 %collective-permute-start.24 = (bf16[9,128,128]{2,1,0:T(8,128)(2,1)}, bf16[9,128,128]{2,1,0:T(8,128)(2,1)}, u32[]{:S(2)}, u32[]{:S(2)}) collective-permute-start(bf16[9,128,128]{2,1,0:T(8,128)(2,1)} %get-tuple-element.63), channel_id=1, source_target_pairs={{0,16},{4,20},{8,24},{12,28},{16,0},{20,4},{24,8},{28,12},{1,17},{... | collective-permute-start | bytes 884744 | tf_op jit(solution)/shard_map/ppermute | solution.py:366
  124.5 17.6 %collective-permute-start.25 = (bf16[9,128,128]{2,1,0:T(8,128)(2,1)}, bf16[9,128,128]{2,1,0:T(8,128)(2,1)}, u32[]{:S(2)}, u32[]{:S(2)}) collective-permute-start(bf16[9,128,128]{2,1,0:T(8,128)(2,1)} %get-tuple-element.64), channel_id=1, source_target_pairs={{0,24},{4,28},{8,16},{12,20},{16,8},{20,12},{24,0},{28,4},{1,25},{... | collective-permute-start | bytes 884744 | tf_op jit(solution)/shard_map/ppermute | solution.py:366
  145.9 41.2 %collective-permute-start.26 = (f32[576,384]{1,0:T(8,128)}, f32[576,384]{1,0:T(8,128)}, u32[]{:S(2)}, u32[]{:S(2)}) collective-permute-start(f32[576,384]{1,0:T(8,128)} %get-tuple-element.66), channel_id=1, source_target_pairs={{0,4},{4,0},{8,12},{12,8},{16,20},{20,16},{24,28},{28,24},{1,5},{5... | collective-permute-start | bytes 2654216 | tf_op jit(solution)/shard_map/ppermute | solution.py:30
  168.3 15.7 %collective-permute-start.28 = (bf16[9,128,128]{2,1,0:T(8,128)(2,1)}, bf16[9,128,128]{2,1,0:T(8,128)(2,1)S(1)}, u32[]{:S(2)}, u32[]{:S(2)}) collective-permute-start(bf16[9,128,128]{2,1,0:T(8,128)(2,1)} %get-tuple-element.71), channel_id=1, source_target_pairs={{0,16},{4,20},{8,24},{12,28},{16,0},{20,4},{24,8},{28,12},{1,17},{... | collective-permute-start | bytes 884744 | tf_op jit(solution)/shard_map/ppermute | solution.py:366
  168.7 15.3 %collective-permute-start.29 = (bf16[9,128,128]{2,1,0:T(8,128)(2,1)}, bf16[9,128,128]{2,1,0:T(8,128)(2,1)S(1)}, u32[]{:S(2)}, u32[]{:S(2)}) collective-permute-start(bf16[9,128,128]{2,1,0:T(8,128)(2,1)} %get-tuple-element.72), channel_id=1, source_target_pairs={{0,24},{4,28},{8,16},{12,20},{16,8},{20,12},{24,0},{28,4},{1,25},{... | collective-permute-start | bytes 884744 | tf_op jit(solution)/shard_map/ppermute | solution.py:366
  (30 other events, 338.6 us)
